TPU v7x, 32 devices: a whole 2x2x4 slice. The times are simulated.
32 devices in a mesh: section: 4 (over z), dp: 8 (over y, x, core).
Axes of the slice: x: 2, y: 2, z: 4, core: 2. Of those that a mesh axis runs over, the one named last changes fastest.
Arguments:
- patches: bfloat16 [8192, 1280], P('dp'), may hold values from -6 to 6
- pre_gain: float32 [1280], replicated, may hold values from 0.1 to 1.9
- merge_gain: float32 [1280], replicated, may hold values from 0.1 to 1.9
- merge_bias: float32 [1280], replicated, may hold values from -3 to 3
- w_in: bfloat16 [1280, 2560], P('dp', 'section'), may hold values from -0.15625 to 0.15625
- w_out: bfloat16 [2560, 1280], P('section', 'dp'), may hold values from -0.125 to 0.125
- destinations: int32 [2048, 1], P(('section', 'dp')), may hold values from 0 to 7; in each aligned block of 64 rows (0 to 63, 64 to 127, ...) at most 8 rows name the same one
- upstream: bfloat16 [2048, 5120], P(('section', 'dp')), may hold values from -6 to 6
Outputs:
- received: bfloat16 [2048, 5120], P(('section', 'dp'))
- grad_w_in: float32 [1280, 2560], P('dp', 'section')
- grad_w_out: float32 [2560, 1280], P('section', 'dp')
Inputs may be any that keep to these rules, and one draw needn't show every extreme that they name: `destinations`: among the 64 blocks of one device, one replica is named at most 8 times, and exactly 8 times for some replica in some devices.
All inputs are finite; a program needn't handle non-finite values.
Results may differ from a plain program's by a relative error of at most 0.0068.
Values may be sent and summed in bfloat16 or wider, within the bound.
A program may use at most 128 MiB of HBM per device.

v0:
```python
import jax
import jax.numpy as jnp
from jax import lax
from jax.sharding import PartitionSpec as P

BLK = 1


epsilon = 1e-06
gelu_scale = 0.7978845608028654
gelu_cubic = 0.044715


def gelu_slope(values):
    tangent = jnp.tanh(gelu_scale * (values + gelu_cubic * values * values * values))
    return 0.5 * (1.0 + tangent) + 0.5 * values * (1.0 - tangent * tangent) * gelu_scale * (
        1.0 + 3.0 * gelu_cubic * values * values
    )


def normalize(values):
    average = jnp.mean(values, axis=-1, keepdims=True)
    centred = values - average
    inv_scale = lax.rsqrt(jnp.mean(centred * centred, axis=-1, keepdims=True) + epsilon)
    return (centred * inv_scale, inv_scale)


def norm_backward(cotangent, unit_rows, inv_scale, gain):
    scaled = cotangent * gain
    return inv_scale * (
        scaled
        - jnp.mean(scaled, axis=-1, keepdims=True)
        - unit_rows * jnp.mean(scaled * unit_rows, axis=-1, keepdims=True)
    )


def block_ranks(targets):
    block_count = targets.shape[-1]
    matches = targets[:, None] == targets[None, :]
    earlier = lax.broadcasted_iota(jnp.int32, (block_count, block_count), 1) < lax.broadcasted_iota(
        jnp.int32, (block_count, block_count), 0
    )
    return jnp.sum((matches & earlier).astype(jnp.int32), axis=-1)


def on_device(patches, pre_gain, merge_gain, merge_bias, w_in, w_out, destinations, upstream):
    sections = lax.axis_size("section")
    replicas = lax.axis_size("dp")
    group_rows = patches.shape[0]
    share_rows = group_rows // sections
    feature_count = patches.shape[1]
    merged_width = upstream.shape[1]
    block_width = BLK * merged_width
    block_count = destinations.shape[0]
    capacity = upstream.shape[0] // (replicas * BLK)
    inputs = patches.astype(jnp.float32)
    unit_rows, _ = normalize(inputs)
    normed = (unit_rows * pre_gain).astype(jnp.bfloat16)
    preact = jnp.dot(
        normed, lax.all_gather(w_in, "dp", axis=0, tiled=True), preferred_element_type=jnp.float32
    )
    hidden = jax.nn.gelu(preact, approximate=True).astype(jnp.bfloat16)
    out_full = lax.all_gather(w_out, "dp", axis=1, tiled=True)
    partial_value = jnp.dot(hidden, out_full, preferred_element_type=jnp.float32)
    row_start = lax.axis_index("section") * share_rows
    own_inputs = lax.dynamic_slice_in_dim(inputs, row_start, share_rows, 0)
    residual = own_inputs + lax.psum_scatter(
        partial_value, "section", scatter_dimension=0, tiled=True
    )
    unit_out, scale_out = normalize(residual)
    merged = (unit_out * merge_gain + merge_bias).astype(jnp.bfloat16)
    blocks = merged.reshape(block_count, block_width)
    targets = destinations[:, 0]
    block_rank = block_ranks(targets)
    column_ids = lax.broadcasted_iota(jnp.int32, (block_count, replicas * capacity), 1)
    picker = ((targets * capacity + block_rank)[:, None] == column_ids).astype(jnp.bfloat16)
    outgoing = lax.dot_general(
        picker, blocks, (((0,), (0,)), ((), ())), preferred_element_type=jnp.float32
    ).astype(jnp.bfloat16)
    arrived = lax.all_to_all(
        outgoing.reshape(replicas, capacity * block_width),
        "dp",
        split_axis=0,
        concat_axis=0,
        tiled=True,
    )
    received = arrived.reshape(replicas * capacity * BLK, merged_width)
    coming = lax.all_to_all(
        upstream.reshape(replicas, capacity * block_width),
        "dp",
        split_axis=0,
        concat_axis=0,
        tiled=True,
    )
    cotangent = jnp.dot(
        picker, coming.reshape(replicas * capacity, block_width), preferred_element_type=jnp.float32
    )
    cotangent = cotangent.astype(jnp.bfloat16).reshape(share_rows, feature_count)
    grad_own = norm_backward(cotangent.astype(jnp.float32), unit_out, scale_out, merge_gain).astype(
        jnp.bfloat16
    )
    grad_residual = lax.all_gather(grad_own, "section", axis=0, tiled=True)
    grad_second = lax.dot_general(
        hidden, grad_residual, (((0,), (0,)), ((), ())), preferred_element_type=jnp.float32
    )
    grad_hidden = lax.dot_general(
        grad_residual, out_full, (((1,), (1,)), ((), ())), preferred_element_type=jnp.float32
    )
    grad_preact = (grad_hidden * gelu_slope(preact)).astype(jnp.bfloat16)
    grad_first = lax.dot_general(
        normed, grad_preact, (((0,), (0,)), ((), ())), preferred_element_type=jnp.float32
    )
    grad_w_in, grad_w_out = (
        lax.psum_scatter(grad_first, "dp", scatter_dimension=0, tiled=True),
        lax.psum_scatter(grad_second, "dp", scatter_dimension=1, tiled=True),
    )
    return (received, grad_w_in, grad_w_out)


def solution(mesh):
    return jax.shard_map(
        on_device,
        mesh=mesh,
        in_specs=(
            P("dp", None),
            P(),
            P(),
            P(),
            P("dp", "section"),
            P("section", "dp"),
            P(("section", "dp"), None),
            P(("section", "dp"), None),
        ),
        out_specs=(P(("section", "dp"), None), P("dp", "section"), P("section", "dp")),
        check_vma=False,
    )
```

profile of v0, /device:TPU:0, one launch (start us, length us, event | category | flops | bytes accessed | tf_op | source)
XLA Modules:
  0.0 343.3 jit_solution(11748696591009729824)
XLA Ops:
  7.2 0.0 all-gather.4.cloned.1.call-start
  7.2 0.7 all-gather.4.cloned.1.call-update
  7.9 0.0 all-gather.6.cloned.1.call-start
  8.0 0.7 all-gather.6.cloned.1.call-update
  8.7 0.0 reduce-scatter.4.cloned.1.call-start
  8.7 2.2 convert_reduce_fusion
  10.9 0.8 multiply_reduce_fusion
  11.7 26.7 %all-gather.4.cloned.1.call-done = bf16[1280,640]{1,0:T(8,128)(2,1)} async-done(((bf16[160,640]{1,0:T(8,128)(2,1)}), bf16[1280,640]{1,0:T(8,128)(2,1)}) %all-gather.4.cloned.1.call-update) | async-done | bytes 1638416 | tf_op jit(solution)/shard_map/all_gather | solution.py:60
  38.5 5.3 %fusion.30 = f32[1024,640]{1,0:T(8,128)} fusion(bf16[1280,640]{1,0:T(8,128)(2,1)} %all-gather.4.cloned.1.call-done, bf16[1024,1280]{1,0:T(8,128)(2,1)S(1)} %copy-done, f32[1280]{0:T(1024)S(1)} %copy-done.6, f32[1024]{0:T(1024)S(1)} %add_rsqrt_fusion, f32[1024]{0:T(1024)S(1)} %broadcast_multiply_fusion), kind=kOutput, calls=%fused_computation.53 | convolution fusion | flops 1684275200 | bytes 6894592 | tf_op jit(solution)/shard_map/dot_general | solution.py:59
  43.8 22.5 %all-gather.6.cloned.1.call-done = bf16[640,1280]{0,1:T(8,128)(2,1)} async-done(((bf16[640,160]{0,1:T(8,128)(2,1)}), bf16[640,1280]{0,1:T(8,128)(2,1)}) %all-gather.6.cloned.1.call-update) | async-done | bytes 1638416 | tf_op jit(solution)/shard_map/all_gather | solution.py:63
  66.2 7.2 %fusion.28 = f32[1024,1280]{1,0:T(8,128)} fusion(bf16[640,1280]{0,1:T(8,128)(2,1)} %all-gather.6.cloned.1.call-done, f32[1024,640]{1,0:T(8,128)} %fusion.30), kind=kOutput, calls=%fused_computation.52 | convolution fusion | flops 1683619840 | bytes 9502720 | tf_op jit(solution)/shard_map/dot_general | solution.py:64
  73.4 1.1 copy-done.2
  74.5 1.8 all_to_all.17
  76.3 0.5 broadcast.106
  76.8 5.7 %reduce.2 = bf16[8,40960]{1,0:T(8,128)(2,1)S(1)} reduce(bf16[8,1,40960]{2,1,0:T(2,128)(2,1)} %all_to_all.17, bf16[]{:T(256)} %broadcast.106), dimensions={1}, to_apply=%all_to_all.17.reduce_sub_computation | reduce | bytes 1310722 | tf_op jit(solution)/shard_map/all_to_all | solution.py:88
  82.5 1.3 reshape.73
  83.8 3.5 %all-to-all-start.1 = ((bf16[8,2,20480]{2,1,0:T(2,128)(2,1)}), bf16[8,2,20480]{2,1,0:T(2,128)(2,1)S(1)}, u32[]{:S(2)}, u32[]{:S(2)}) async-start(bf16[8,2,20480]{2,1,0:T(2,128)(2,1)} %reshape.73), calls=%async_computation.2 | async-start | bytes 1310720 | tf_op jit(solution)/shard_map/all_to_all | solution.py:88
  87.4 0.2 all-gather.8.cloned.1.call-start
  87.6 2.7 convert_element_type.35
  90.4 0.2 convert_reduce_fusion.1
  90.5 7.9 %all-to-all-done.1 = bf16[8,2,20480]{2,1,0:T(2,128)(2,1)S(1)} async-done(((bf16[8,2,20480]{2,1,0:T(2,128)(2,1)}), bf16[8,2,20480]{2,1,0:T(2,128)(2,1)S(1)}, u32[]{:S(2)}, u32[]{:S(2)}) %all-to-all-start.1) | async-done | bytes 655392 | tf_op jit(solution)/shard_map/all_to_all | solution.py:88
  98.4 1.9 reshape.74
  100.3 5.2 %reduce.1 = bf16[8,40960]{1,0:T(8,128)(2,1)S(1)} reduce(bf16[8,1,40960]{2,1,0:T(2,128)(2,1)} %reshape.74, bf16[]{:T(256)} %constant.37), dimensions={1}, to_apply=%all_to_all.15.reduce_sub_computation | reduce | bytes 1310722 | tf_op jit(solution)/shard_map/all_to_all | solution.py:88
  105.5 1.1 reshape.67
  106.6 2.5 fusion
  109.2 2.7 reshape.68
  111.8 55.5 %reduce-scatter.4.cloned.1.call-done = f32[256,1280]{1,0:T(8,128)} async-done(((f32[1024,1280]{1,0:T(8,128)}), f32[256,1280]{1,0:T(8,128)}) %reduce-scatter.4.cloned.1.call-update) | async-done | bytes 1310736 | tf_op jit(solution)/shard_map/reduce_scatter | solution.py:67
  167.4 2.0 fusion.31
  169.4 0.3 multiply_reduce_fusion.2
  169.7 0.4 multiply_reduce_fusion.3
  170.1 1.4 multiply_convert_fusion.1
  171.5 0.0 reduce-scatter.6.cloned.1.call-start
  171.6 55.4 %all-gather.8.cloned.1.call-done = bf16[1024,1280]{1,0:T(8,128)(2,1)} async-done(((bf16[256,1280]{1,0:T(8,128)(2,1)}), bf16[1024,1280]{1,0:T(8,128)(2,1)}) %all-gather.8.cloned.1.call-update) | async-done | bytes 2621456 | tf_op jit(solution)/shard_map/all_gather | solution.py:102
  226.9 10.2 %fusion.16 = f32[1280,640]{1,0:T(8,128)} fusion(f32[1024,640]{1,0:T(8,128)} %fusion.30, bf16[1024,1280]{1,0:T(8,128)(2,1)} %all-gather.8.cloned.1.call-done, bf16[640,1280]{0,1:T(8,128)(2,1)} %all-gather.6.cloned.1.call-done, bf16[1024,1280]{1,0:T(8,128)(2,1)S(1)} %copy-done, f32[1280]{0:T(1024)S(1)} %copy-done.6, f32[1024]{0:T(1024)S(1)} %add_rsqrt_fusion, ...), kind=kOutput, calls=%fused_computation.31 | convolution fusion | flops 3374448640 | bytes 12792832 | tf_op jit(solution)/shard_map/dot_general | solution.py:110
  237.2 0.3 reduce-scatter.8.cloned.1.call-start
  237.5 1.4 copy-done.5
  238.9 5.9 %fusion.26 = f32[640,1280]{0,1:T(8,128)} fusion(bf16[1024,1280]{1,0:T(8,128)(2,1)S(1)} %copy-done.5, f32[1024,640]{1,0:T(8,128)} %fusion.30), kind=kOutput, calls=%fused_computation.51 | convolution fusion | flops 1683619840 | bytes 8519680 | tf_op jit(solution)/shard_map/dot_general | solution.py:103
  244.8 0.4 reshape.65
  245.2 0.5 convolution_convert_fusion.1
  245.7 0.6 all_to_all.16
  246.2 4.5 %reduce.3 = bf16[8,40960]{1,0:T(8,128)(2,1)S(1)} reduce(bf16[8,1,40960]{2,1,0:T(2,128)(2,1)S(1)} %all_to_all.16, bf16[]{:T(256)} %broadcast.106), dimensions={1}, to_apply=%all_to_all.16.reduce_sub_computation | reduce | bytes 1310722 | tf_op jit(solution)/shard_map/all_to_all | solution.py:80
  250.8 0.5 reshape.71
  251.3 20.3 %all_to_all.20 = bf16[8,2,20480]{2,1,0:T(2,128)(2,1)S(1)} all-to-all(bf16[8,2,20480]{2,1,0:T(2,128)(2,1)S(1)} %reshape.71), channel_id=1, replica_groups=mesh['section'=4,'dp'=8] {'dp'}, dimensions={0} | all-to-all | bytes 1310720 | tf_op jit(solution)/shard_map/all_to_all | solution.py:80
  271.6 0.6 reshape.72
  272.2 4.0 %reduce = bf16[8,40960]{1,0:T(8,128)(2,1)S(1)} reduce(bf16[8,1,40960]{2,1,0:T(2,128)(2,1)S(1)} %reshape.72, bf16[]{:T(256)} %constant.37), dimensions={1}, to_apply=%all_to_all.13.reduce_sub_computation | reduce | bytes 1310722 | tf_op jit(solution)/shard_map/all_to_all | solution.py:80
  276.2 1.1 reshape.66
  277.3 8.5 %reduce-scatter.6.cloned.1.call-done = f32[160,640]{1,0:T(8,128)} async-done(((f32[1280,640]{1,0:T(8,128)}), f32[160,640]{1,0:T(8,128)}) %reduce-scatter.6.cloned.1.call-update) | async-done | bytes 409616 | tf_op jit(solution)/shard_map/reduce_scatter | solution.py:114
  285.9 50.6 %reduce-scatter.8.cloned.1.call-done = f32[640,160]{0,1:T(8,128)} async-done(((f32[640,1280]{0,1:T(8,128)}), f32[640,160]{0,1:T(8,128)}) %reduce-scatter.8.cloned.1.call-update) | async-done | bytes 409616 | tf_op jit(solution)/shard_map/reduce_scatter | solution.py:115
  (24 shorter events, 0.1 us)
Async XLA Ops:
  7.2 3.7 %copy-start = (bf16[1024,1280]{1,0:T(8,128)(2,1)S(1)}, bf16[1024,1280]{1,0:T(8,128)(2,1)}, u32[]{:S(2)}) copy-start(bf16[1024,1280]{1,0:T(8,128)(2,1)} %param.8) | copy-start | bytes 7864324
  7.2 31.3 %all-gather.4.cloned.1.call-start = ((), (), s32[]{:S(2)}) async-start(), calls=%async_computation.5 | async-start | bytes 1843200 | tf_op jit(solution)/shard_map/all_gather | solution.py:60
  7.9 58.3 %all-gather.6.cloned.1.call-start = ((), (), s32[]{:S(2)}) async-start(), calls=%async_computation.6 | async-start | bytes 1843200 | tf_op jit(solution)/shard_map/all_gather | solution.py:63
  8.7 29.8 %copy-start.6 = (f32[1280]{0:T(1024)S(1)}, f32[1280]{0:T(1024)}, u32[]{:S(2)}) copy-start(f32[1280]{0:T(1024)} %param.9) | copy-start | bytes 15364
  8.7 158.7 %reduce-scatter.4.cloned.1.call-start = ((), (), s32[]{:S(2)}) async-start(), calls=%async_computation.7 | async-start | bytes 6553600 | tf_op jit(solution)/shard_map/reduce_scatter | solution.py:67
  73.4 1.1 copy-start.2
  83.8 14.6 %all-to-all-start.1 = ((bf16[8,2,20480]{2,1,0:T(2,128)(2,1)}), bf16[8,2,20480]{2,1,0:T(2,128)(2,1)S(1)}, u32[]{:S(2)}, u32[]{:S(2)}) async-start(bf16[8,2,20480]{2,1,0:T(2,128)(2,1)} %reshape.73), calls=%async_computation.2 | async-start | bytes 1310720 | tf_op jit(solution)/shard_map/all_to_all | solution.py:88
  87.4 139.6 %all-gather.8.cloned.1.call-start = ((), (), s32[]{:S(2)}) async-start(), calls=%async_computation.8 | async-start | bytes 3276800 | tf_op jit(solution)/shard_map/all_gather | solution.py:102
  87.6 2.8 copy-start.7
  111.8 57.9 %copy-start.3 = (f32[1280]{0:T(1024)S(1)}, f32[1280]{0:T(1024)}, u32[]{:S(2)}) copy-start(f32[1280]{0:T(1024)} %param.10) | copy-start | bytes 15364
  167.4 2.4 copy-start.1
  169.4 0.7 copy-start.4
  171.5 114.3 %reduce-scatter.6.cloned.1.call-start = ((), (), s32[]{:S(2)}) async-start(), calls=%async_computation.9 | async-start | bytes 3686400 | tf_op jit(solution)/shard_map/reduce_scatter | solution.py:114
  237.2 1.7 copy-start.5
  237.2 99.3 %reduce-scatter.8.cloned.1.call-start = ((), (), s32[]{:S(2)}) async-start(), calls=%async_computation.10 | async-start | bytes 3686400 | tf_op jit(solution)/shard_map/reduce_scatter | solution.py:115
Sparse Core Ops, SparseCore 0:
  9.9 28.5 all-gather.3
  40.3 25.8 all-gather.5
  73.5 93.7 reduce-scatter.3
  171.6 55.2 all-gather.7
  237.3 48.4 reduce-scatter.5
  289.7 46.7 reduce-scatter.7
where the time goes:
time: 344 us; the launch traced here: 343 us
  waiting for transfers between devices  229 us (67%)
  matrix products  31.6 us (9%)
  other arithmetic  29.3 us (9%)
  blocking collectives  20.3 us (6%)
  local copies, waits for them, and re-layouts  15.1 us (4%)
  between operations  14.3 us (4%)
  starting transfers between devices  4.18 us (1%)
    reduce_scatter x1, waiting for transfers between devices, on_device(): lax.psum_scatter(partial_value, 'section', scatter_dimension=0, tiled=True)  55.5 us
    all_gather x1, waiting for transfers between devices, on_device(): grad_residual = lax.all_gather(grad_own, 'section', axis=0, tiled=True)  55.4 us
    reduce_scatter x1, waiting for transfers between devices, on_device(): lax.psum_scatter(grad_second, 'dp', scatter_dimension=1, tiled=True)  50.6 us
    all_gather x1, waiting for transfers between devices, on_device(): lax.all_gather(w_in, 'dp', axis=0, tiled=True)  26.7 us
    all_gather x1, waiting for transfers between devices, on_device(): out_full = lax.all_gather(w_out, 'dp', axis=1, tiled=True)  22.5 us
    all_to_all x1, blocking collectives, on_device(): lax.all_to_all(outgoing.reshape(replicas, capacity * block_width), 'dp',...  20.3 us
    all_to_all x2, other arithmetic, on_device(): lax.all_to_all(upstream.reshape(replicas, capacity * block_width), 'dp',...  10.8 us
    dot_general x1, matrix products, on_device(): lax.dot_general(normed, grad_preact, (((0,), (0,)), ((), ())), preferred_...  10.2 us
  transfers between devices with their start and end apart: 7, of which 7 were waited for; matrix products, arithmetic and copies ran while one was open for 14% of the time, Pallas kernels for 0%

commit v1 on v0

--- a/solution.py
+++ b/solution.py
@@ -61,12 +61,12 @@
     )
     hidden = jax.nn.gelu(preact, approximate=True).astype(jnp.bfloat16)
     out_full = lax.all_gather(w_out, "dp", axis=1, tiled=True)
-    partial_value = jnp.dot(hidden, out_full, preferred_element_type=jnp.float32)
+    partial_value = jnp.dot(hidden, out_full, preferred_element_type=jnp.float32).astype(jnp.bfloat16)
     row_start = lax.axis_index("section") * share_rows
     own_inputs = lax.dynamic_slice_in_dim(inputs, row_start, share_rows, 0)
     residual = own_inputs + lax.psum_scatter(
         partial_value, "section", scatter_dimension=0, tiled=True
-    )
+    ).astype(jnp.float32)
     unit_out, scale_out = normalize(residual)
     merged = (unit_out * merge_gain + merge_bias).astype(jnp.bfloat16)
     blocks = merged.reshape(block_count, block_width)
@@ -111,8 +111,8 @@
         normed, grad_preact, (((0,), (0,)), ((), ())), preferred_element_type=jnp.float32
     )
     grad_w_in, grad_w_out = (
-        lax.psum_scatter(grad_first, "dp", scatter_dimension=0, tiled=True),
-        lax.psum_scatter(grad_second, "dp", scatter_dimension=1, tiled=True),
+        lax.psum_scatter(grad_first.astype(jnp.bfloat16), "dp", scatter_dimension=0, tiled=True).astype(jnp.float32),
+        lax.psum_scatter(grad_second.astype(jnp.bfloat16), "dp", scatter_dimension=1, tiled=True).astype(jnp.float32),
     )
     return (received, grad_w_in, grad_w_out)
 

time: 344 us -> 285 us (0.83)
  waiting for transfers between devices: 229 us -> 170 us
    reduce_scatter x1, waiting for transfers between devices: 55.5 us -> 13.7 us  [on_device(): lax.psum_scatter(partial_value, 'section', scatter_dimension=0, tiled=True)]
    reduce_scatter x2, waiting for transfers between devices: 59.1 us -> 43.1 us  [the longest x1 40.1 us: on_device(): lax.psum_scatter(grad_second.astype(jnp.bfloat16), 'dp', scatter_dimensio...]
    unnamed x20 -> x18, local copies, waits for them, and re-layouts: 6.92 us -> 5.52 us
  transfers between devices with their start and end apart: 7 -> 7, of which waited for: 7 -> 7; matrix products, arithmetic and copies ran while one was open for 14% -> 18% of each run, Pallas kernels for 0% -> 0%
where the time goes in v1:
time: 285 us; the launch traced here: 284 us
  waiting for transfers between devices  170 us (60%)
  other arithmetic  32.7 us (11%)
  matrix products  30.6 us (11%)
  blocking collectives  19 us (7%)
  between operations  14.3 us (5%)
  local copies, waits for them, and re-layouts  13.8 us (5%)
  starting transfers between devices  4.18 us (1%)
    all_gather x1, waiting for transfers between devices, on_device(): grad_residual = lax.all_gather(grad_own, 'section', axis=0, tiled=True)  54.4 us
    reduce_scatter x1, waiting for transfers between devices, on_device(): lax.psum_scatter(grad_second.astype(jnp.bfloat16), 'dp', scatter_dimensio...  40.1 us
    all_gather x1, waiting for transfers between devices, on_device(): lax.all_gather(w_in, 'dp', axis=0, tiled=True)  26.7 us
    all_gather x1, waiting for transfers between devices, on_device(): out_full = lax.all_gather(w_out, 'dp', axis=1, tiled=True)  22.5 us
    all_to_all x1, blocking collectives, on_device(): lax.all_to_all(outgoing.reshape(replicas, capacity * block_width), 'dp',...  19 us
    reduce_scatter x1, waiting for transfers between devices, on_device(): lax.psum_scatter(partial_value, 'section', scatter_dimension=0, tiled=True)  13.7 us
    all_to_all x2, other arithmetic, on_device(): lax.all_to_all(upstream.reshape(replicas, capacity * block_width), 'dp',...  11 us
    dot_general x1, matrix products, on_device(): lax.dot_general(normed, grad_preact, (((0,), (0,)), ((), ())), preferred_...  9.76 us
  transfers between devices with their start and end apart: 7, of which 7 were waited for; matrix products, arithmetic and copies ran while one was open for 18% of the time, Pallas kernels for 0%

profile of v1, /device:TPU:0, one launch (start us, length us, event | category | flops | bytes accessed | tf_op | source)
XLA Modules:
  0.0 284.5 jit_solution(13928924853613796800)
XLA Ops:
  7.2 0.7 all-gather.4.cloned.1.call-update
  7.9 0.0 all-gather.6.cloned.1.call-start
  8.0 0.7 all-gather.6.cloned.1.call-update
  8.7 0.0 reduce-scatter.4.cloned.1.call-start
  8.7 2.2 convert_reduce_fusion
  10.9 0.8 multiply_reduce_fusion
  11.7 26.7 %all-gather.4.cloned.1.call-done = bf16[1280,640]{1,0:T(8,128)(2,1)} async-done(((bf16[160,640]{1,0:T(8,128)(2,1)}), bf16[1280,640]{1,0:T(8,128)(2,1)}) %all-gather.4.cloned.1.call-update) | async-done | bytes 1638416 | tf_op jit(solution)/shard_map/all_gather | solution.py:60
  38.5 5.3 %fusion.27 = f32[1024,640]{1,0:T(8,128)} fusion(bf16[1280,640]{1,0:T(8,128)(2,1)} %all-gather.4.cloned.1.call-done, bf16[1024,1280]{1,0:T(8,128)(2,1)S(1)} %copy-done, f32[1280]{0:T(1024)S(1)} %copy-done.5, f32[1024]{0:T(1024)S(1)} %add_rsqrt_fusion, f32[1024]{0:T(1024)S(1)} %broadcast_multiply_fusion), kind=kOutput, calls=%fused_computation.53 | convolution fusion | flops 1684275200 | bytes 6894592 | tf_op jit(solution)/shard_map/dot_general | solution.py:59
  43.8 22.5 %all-gather.6.cloned.1.call-done = bf16[640,1280]{0,1:T(8,128)(2,1)} async-done(((bf16[640,160]{0,1:T(8,128)(2,1)}), bf16[640,1280]{0,1:T(8,128)(2,1)}) %all-gather.6.cloned.1.call-update) | async-done | bytes 1638416 | tf_op jit(solution)/shard_map/all_gather | solution.py:63
  66.2 6.4 %convolution_convert_fusion.2 = bf16[1024,1280]{1,0:T(8,128)(2,1)} fusion(bf16[640,1280]{0,1:T(8,128)(2,1)} %all-gather.6.cloned.1.call-done, f32[1024,640]{1,0:T(8,128)} %fusion.27), kind=kOutput, calls=%fused_computation.9 | convolution fusion | flops 1684930560 | bytes 6881280 | tf_op jit(solution)/shard_map/dot_general | solution.py:64
  72.7 1.1 copy-done.2
  73.7 1.8 all_to_all.17
  75.6 0.5 broadcast.106
  76.1 5.8 %reduce.2 = bf16[8,40960]{1,0:T(8,128)(2,1)S(1)} reduce(bf16[8,1,40960]{2,1,0:T(2,128)(2,1)} %all_to_all.17, bf16[]{:T(256)} %broadcast.106), dimensions={1}, to_apply=%all_to_all.17.reduce_sub_computation | reduce | bytes 1310722 | tf_op jit(solution)/shard_map/all_to_all | solution.py:88
  81.9 1.3 reshape.73
  83.2 3.5 %all-to-all-start.1 = ((bf16[8,2,20480]{2,1,0:T(2,128)(2,1)}), bf16[8,2,20480]{2,1,0:T(2,128)(2,1)S(1)}, u32[]{:S(2)}, u32[]{:S(2)}) async-start(bf16[8,2,20480]{2,1,0:T(2,128)(2,1)} %reshape.73), calls=%async_computation.2 | async-start | bytes 1310720 | tf_op jit(solution)/shard_map/all_to_all | solution.py:88
  86.8 0.2 all-gather.8.cloned.1.call-start
  87.0 2.7 convert_element_type.53
  89.7 0.2 convert_reduce_fusion.1
  89.9 7.9 %all-to-all-done.1 = bf16[8,2,20480]{2,1,0:T(2,128)(2,1)S(1)} async-done(((bf16[8,2,20480]{2,1,0:T(2,128)(2,1)}), bf16[8,2,20480]{2,1,0:T(2,128)(2,1)S(1)}, u32[]{:S(2)}, u32[]{:S(2)}) %all-to-all-start.1) | async-done | bytes 655392 | tf_op jit(solution)/shard_map/all_to_all | solution.py:88
  97.8 1.9 reshape.74
  99.8 5.2 %reduce.1 = bf16[8,40960]{1,0:T(8,128)(2,1)S(1)} reduce(bf16[8,1,40960]{2,1,0:T(2,128)(2,1)} %reshape.74, bf16[]{:T(256)} %constant.37), dimensions={1}, to_apply=%all_to_all.15.reduce_sub_computation | reduce | bytes 1310722 | tf_op jit(solution)/shard_map/all_to_all | solution.py:88
  104.9 1.1 reshape.67
  106.1 2.5 fusion
  108.6 2.7 reshape.68
  111.3 13.7 %reduce-scatter.4.cloned.1.call-done = bf16[256,1280]{1,0:T(8,128)(2,1)} async-done(((bf16[1024,1280]{1,0:T(8,128)(2,1)}), bf16[256,1280]{1,0:T(8,128)(2,1)}) %reduce-scatter.4.cloned.1.call-update) | async-done | bytes 655376 | tf_op jit(solution)/shard_map/reduce_scatter | solution.py:67
  125.1 1.8 fusion.28
  126.9 0.3 multiply_reduce_fusion.2
  127.2 0.4 multiply_reduce_fusion.3
  127.7 1.4 multiply_convert_fusion.1
  129.1 0.0 reduce-scatter.6.cloned.1.call-start
  129.1 54.4 %all-gather.8.cloned.1.call-done = bf16[1024,1280]{1,0:T(8,128)(2,1)} async-done(((bf16[256,1280]{1,0:T(8,128)(2,1)}), bf16[1024,1280]{1,0:T(8,128)(2,1)}) %all-gather.8.cloned.1.call-update) | async-done | bytes 2621456 | tf_op jit(solution)/shard_map/all_gather | solution.py:102
  183.5 9.8 %convolution_convert_fusion.4 = bf16[1280,640]{1,0:T(8,128)(2,1)} fusion(f32[1024,640]{1,0:T(8,128)} %fusion.27, bf16[1024,1280]{1,0:T(8,128)(2,1)} %all-gather.8.cloned.1.call-done, bf16[640,1280]{0,1:T(8,128)(2,1)} %all-gather.6.cloned.1.call-done, bf16[1024,1280]{1,0:T(8,128)(2,1)S(1)} %copy-done, f32[1280]{0:T(1024)S(1)} %copy-done.5, ...), kind=kOutput, calls=%fused_computation.11 | convolution fusion | flops 3375267840 | bytes 11154432 | tf_op jit(solution)/shard_map/dot_general | solution.py:110
  193.3 0.3 reduce-scatter.8.cloned.1.call-start
  193.6 6.2 %convolution_convert_fusion.3 = bf16[640,1280]{0,1:T(8,128)(2,1)} fusion(bf16[1024,1280]{1,0:T(8,128)(2,1)} %all-gather.8.cloned.1.call-done, f32[1024,640]{1,0:T(8,128)} %fusion.27), kind=kOutput, calls=%fused_computation.10 | convolution fusion | flops 1684439040 | bytes 6881280 | tf_op jit(solution)/shard_map/dot_general | solution.py:103
  199.8 0.4 reshape.65
  200.2 0.5 convolution_convert_fusion.1
  200.7 0.6 all_to_all.16
  201.2 4.6 %reduce.3 = bf16[8,40960]{1,0:T(8,128)(2,1)S(1)} reduce(bf16[8,1,40960]{2,1,0:T(2,128)(2,1)S(1)} %all_to_all.16, bf16[]{:T(256)} %broadcast.106), dimensions={1}, to_apply=%all_to_all.16.reduce_sub_computation | reduce | bytes 1310722 | tf_op jit(solution)/shard_map/all_to_all | solution.py:80
  205.9 0.5 reshape.71
  206.4 19.0 %all_to_all.20 = bf16[8,2,20480]{2,1,0:T(2,128)(2,1)S(1)} all-to-all(bf16[8,2,20480]{2,1,0:T(2,128)(2,1)S(1)} %reshape.71), channel_id=1, replica_groups=mesh['section'=4,'dp'=8] {'dp'}, dimensions={0} | all-to-all | bytes 1310720 | tf_op jit(solution)/shard_map/all_to_all | solution.py:80
  225.3 0.6 reshape.72
  226.0 4.0 %reduce = bf16[8,40960]{1,0:T(8,128)(2,1)S(1)} reduce(bf16[8,1,40960]{2,1,0:T(2,128)(2,1)S(1)} %reshape.72, bf16[]{:T(256)} %constant.37), dimensions={1}, to_apply=%all_to_all.13.reduce_sub_computation | reduce | bytes 1310722 | tf_op jit(solution)/shard_map/all_to_all | solution.py:80
  230.0 1.1 reshape.66
  231.1 3.0 %reduce-scatter.6.cloned.1.call-done = bf16[160,640]{1,0:T(8,128)(2,1)} async-done(((bf16[1280,640]{1,0:T(8,128)(2,1)}), bf16[160,640]{1,0:T(8,128)(2,1)}) %reduce-scatter.6.cloned.1.call-update) | async-done | bytes 204816 | tf_op jit(solution)/shard_map/reduce_scatter | solution.py:114
  234.1 1.7 convert_element_type.66
  235.8 40.1 %reduce-scatter.8.cloned.1.call-done = bf16[640,160]{0,1:T(8,128)(2,1)} async-done(((bf16[640,1280]{0,1:T(8,128)(2,1)}), bf16[640,160]{0,1:T(8,128)(2,1)}) %reduce-scatter.8.cloned.1.call-update) | async-done | bytes 204816 | tf_op jit(solution)/shard_map/reduce_scatter | solution.py:115
  275.9 1.7 convert_element_type.68
  (24 shorter events, 0.2 us)
Async XLA Ops:
  7.2 3.7 %copy-start = (bf16[1024,1280]{1,0:T(8,128)(2,1)S(1)}, bf16[1024,1280]{1,0:T(8,128)(2,1)}, u32[]{:S(2)}) copy-start(bf16[1024,1280]{1,0:T(8,128)(2,1)} %param.8) | copy-start | bytes 7864324
  7.2 31.3 %all-gather.4.cloned.1.call-start = ((), (), s32[]{:S(2)}) async-start(), calls=%async_computation.5 | async-start | bytes 1843200 | tf_op jit(solution)/shard_map/all_gather | solution.py:60
  7.9 58.3 %all-gather.6.cloned.1.call-start = ((), (), s32[]{:S(2)}) async-start(), calls=%async_computation.6 | async-start | bytes 1843200 | tf_op jit(solution)/shard_map/all_gather | solution.py:63
  8.7 29.8 %copy-start.5 = (f32[1280]{0:T(1024)S(1)}, f32[1280]{0:T(1024)}, u32[]{:S(2)}) copy-start(f32[1280]{0:T(1024)} %param.9) | copy-start | bytes 15364
  8.7 116.4 %reduce-scatter.4.cloned.1.call-start = ((), (), s32[]{:S(2)}) async-start(), calls=%async_computation.7 | async-start | bytes 3276800 | tf_op jit(solution)/shard_map/reduce_scatter | solution.py:67
  72.7 1.1 copy-start.2
  83.2 14.6 %all-to-all-start.1 = ((bf16[8,2,20480]{2,1,0:T(2,128)(2,1)}), bf16[8,2,20480]{2,1,0:T(2,128)(2,1)S(1)}, u32[]{:S(2)}, u32[]{:S(2)}) async-start(bf16[8,2,20480]{2,1,0:T(2,128)(2,1)} %reshape.73), calls=%async_computation.2 | async-start | bytes 1310720 | tf_op jit(solution)/shard_map/all_to_all | solution.py:88
  86.8 96.7 %all-gather.8.cloned.1.call-start = ((), (), s32[]{:S(2)}) async-start(), calls=%async_computation.8 | async-start | bytes 3276800 | tf_op jit(solution)/shard_map/all_gather | solution.py:102
  87.0 2.7 copy-start.6
  111.3 15.9 %copy-start.3 = (f32[1280]{0:T(1024)S(1)}, f32[1280]{0:T(1024)}, u32[]{:S(2)}) copy-start(f32[1280]{0:T(1024)} %param.10) | copy-start | bytes 15364
  125.1 2.1 copy-start.1
  126.9 0.7 copy-start.4
  129.1 105.0 %reduce-scatter.6.cloned.1.call-start = ((), (), s32[]{:S(2)}) async-start(), calls=%async_computation.9 | async-start | bytes 1843200 | tf_op jit(solution)/shard_map/reduce_scatter | solution.py:114
  193.3 82.6 %reduce-scatter.8.cloned.1.call-start = ((), (), s32[]{:S(2)}) async-start(), calls=%async_computation.10 | async-start | bytes 1843200 | tf_op jit(solution)/shard_map/reduce_scatter | solution.py:115
Sparse Core Ops, SparseCore 0:
  9.9 28.5 all-gather.3
  40.4 25.8 all-gather.5
  72.8 52.2 reduce-scatter.3
  129.2 54.3 all-gather.7
  193.4 40.5 reduce-scatter.5
  237.3 38.6 reduce-scatter.7

commit v2 on v1

--- a/solution.py
+++ b/solution.py
@@ -1,6 +1,11 @@
+import functools
+
 import jax
 import jax.numpy as jnp
+import numpy as np
 from jax import lax
+from jax.experimental import pallas as pl
+from jax.experimental.pallas import tpu as pltpu
 from jax.sharding import PartitionSpec as P
 
 BLK = 1
@@ -117,9 +122,403 @@
     return (received, grad_w_in, grad_w_out)
 
 
+TILE = 32
+
+
+def remote(src, dst, send_sem, recv_sem, device):
+    return pltpu.make_async_remote_copy(
+        src_ref=src,
+        dst_ref=dst,
+        send_sem=send_sem,
+        recv_sem=recv_sem,
+        device_id=device,
+        device_id_type=pl.DeviceIdType.MESH,
+    )
+
+
+def window_kernel(
+    sections, replicas, merge, capacity,
+    patches, pre_gain, merge_gain, merge_bias, w_in, w_out_t, tcol, trow, bcol, brow, mcol, mrow, upstream,
+    received, grad_in, grad_out,
+    rows_in, normed, normed_t, first, second, slope, hidden, part_out, part_in, unit, inv, merged, outgoing,
+    coming, cot, grad_rows, grad_rows_t, grad_pre, core_out, core_in, chip_out, chip_in, total, cross_out,
+    cross_in, local_sem, gs, gr, us, ur, os_, or_, ps, pr, xs, xr, cs, cr, hs, hr, zs, zr,
+):
+    share = rows_in.shape[0] // 2
+    features = rows_in.shape[1]
+    width = w_in.shape[1]
+    shard = w_in.shape[0]
+    chips = replicas // 2
+    f32, bf16 = jnp.float32, jnp.bfloat16
+    s, d = lax.axis_index("section"), lax.axis_index("dp")
+    q, c = d // 2, d % 2
+    pair = (s + 1 - 2 * (s % 2), d)
+    across = ((s + sections // 2) % sections, d)
+    mate_core = 1 - c
+    mate = (s, q * 2 + mate_core)
+
+    def chip_at(k):
+        return (q + k) % chips
+
+    def shard_rows(j):
+        return pl.ds(pl.multiple_of(j * shard, 16), shard)
+
+    sent = []
+
+    def send(*args):
+        copy = remote(*args)
+        copy.start()
+        sent.append(copy)
+
+    def arrive(dst, recv_sem, send_sem):
+        remote(dst, dst, send_sem, recv_sem, mate).wait_recv()
+
+    shards, fulls = (w_in, w_out_t), (first, second)
+    loads = [
+        pltpu.make_async_copy(
+            patches.at[pl.ds(pl.multiple_of(s * share, share), share)], rows_in.at[pl.ds(0, share)], local_sem.at[0]
+        ),
+        pltpu.make_async_copy(
+            patches.at[pl.ds(pl.multiple_of(pair[0] * share, share), share)],
+            rows_in.at[pl.ds(share, share)],
+            local_sem.at[1],
+        ),
+        pltpu.make_async_copy(w_in, first.at[0, shard_rows(d)], local_sem.at[2]),
+        pltpu.make_async_copy(w_out_t, second.at[0, shard_rows(d)], local_sem.at[3]),
+    ]
+    slot_rows = capacity * merge
+    loads.append(
+        pltpu.make_async_copy(
+            upstream.at[pl.ds(pl.multiple_of(d * slot_rows, slot_rows), slot_rows)],
+            coming.at[pl.ds(pl.multiple_of(d * slot_rows, slot_rows), slot_rows)],
+            local_sem.at[4],
+        )
+    )
+    for copy in loads:
+        copy.start()
+
+    barrier = pltpu.get_barrier_semaphore()
+    for k in range(1, replicas):
+        pl.semaphore_signal(
+            barrier, inc=1, device_id=(s, (d + k) % replicas), device_id_type=pl.DeviceIdType.MESH
+        )
+    for peer in (pair, across):
+        pl.semaphore_signal(barrier, inc=1, device_id=peer, device_id_type=pl.DeviceIdType.MESH)
+    pl.semaphore_wait(barrier, replicas + 1)
+
+    for w in range(2):
+        send(shards[w], fulls[w].at[1, shard_rows(d)], gs.at[w, 1, 0], gr.at[w, 1, 0], across)
+
+    def spread(w, b):
+        src = shards[w] if b == 0 else fulls[w].at[1, shard_rows(d)]
+        for k in range(1, chips):
+            send(src, fulls[w].at[b, shard_rows(d)], gs.at[w, b, 1 + k], gr.at[w, b, 1 + k], (s, chip_at(k) * 2 + c))
+        send(src, fulls[w].at[b, shard_rows(d)], gs.at[w, b, 1], gr.at[w, b, 1], mate)
+
+    def relay(w, b):
+        for k in range(1, chips):
+            place = fulls[w].at[b, shard_rows(chip_at(chips - k) * 2 + c)]
+            arrive(place, gr.at[w, b, 1 + k], gs.at[w, b, 1 + k])
+            send(place, place, gs.at[w, b, chips + k], gr.at[w, b, chips + k], mate)
+
+    def gathered(w, b):
+        arrive(fulls[w].at[b, shard_rows(q * 2 + mate_core)], gr.at[w, b, 1], gs.at[w, b, 1])
+        for k in range(1, chips):
+            place = fulls[w].at[b, shard_rows(chip_at(chips - k) * 2 + mate_core)]
+            arrive(place, gr.at[w, b, chips + k], gs.at[w, b, chips + k])
+
+    spread(0, 0)
+    arrive(first.at[1, shard_rows(d)], gr.at[0, 1, 0], gs.at[0, 1, 0])
+    spread(0, 1)
+    spread(1, 0)
+    arrive(second.at[1, shard_rows(d)], gr.at[1, 1, 0], gs.at[1, 1, 0])
+    spread(1, 1)
+    for k in range(1, replicas):
+        peer = (d + k) % replicas
+        send(
+            upstream.at[pl.ds(pl.multiple_of(peer * slot_rows, slot_rows), slot_rows)],
+            coming.at[pl.ds(pl.multiple_of(d * slot_rows, slot_rows), slot_rows)],
+            us.at[k],
+            ur.at[k],
+            (s, peer),
+        )
+
+    for copy in loads:
+        copy.wait()
+
+    def tile_rows(i):
+        return pl.ds(pl.multiple_of(i * TILE, TILE), TILE)
+
+    @pl.loop(0, 2 * share // TILE)
+    def _(i):
+        unit_rows, _ = normalize(rows_in[tile_rows(i), :].astype(f32))
+        normed[tile_rows(i), :] = (unit_rows * pre_gain[...]).astype(bf16)
+
+    def flip(src, dst, r):
+        @pl.loop(0, features // 128)
+        def _(i):
+            cols = pl.ds(pl.multiple_of(i * 128, 128), 128)
+            dst[cols, pl.ds(r * share, share)] = src[pl.ds(r * share, share), cols].T
+
+    relay(0, 0)
+    flip(normed, normed_t, 0)
+    flip(normed, normed_t, 1)
+    relay(0, 1)
+
+    matches = tcol[...] == trow[...]
+    above = jnp.where(matches & (brow[...] < bcol[...]) & (mrow[...] == 0.0), 1.0, 0.0)
+    left = jnp.where(matches & (bcol[...] < brow[...]) & (mcol[...] == 0.0), 1.0, 0.0)
+    slot_col = (tcol[...] * capacity + jnp.sum(above, axis=1, keepdims=True)) * merge + mcol[...]
+    slot_row = (trow[...] * capacity + jnp.sum(left, axis=0, keepdims=True)) * merge + mrow[...]
+    lanes = lax.broadcasted_iota(jnp.int32, (share, share), 1).astype(f32)
+    subs = lax.broadcasted_iota(jnp.int32, (share, share), 0).astype(f32)
+
+    def half(r):
+        return pl.ds(r * share, share)
+
+    for b in range(2):
+        gathered(0, b)
+        for r in range(2):
+            slope[b, half(r), :] = jnp.dot(normed[half(r), :], first[b], preferred_element_type=f32)
+        if b == 0:
+            relay(1, 0)
+
+        @pl.loop(0, 2 * share // TILE)
+        def _(i):
+            u = slope[b, tile_rows(i), :]
+            tangent = jnp.tanh(gelu_scale * (u + gelu_cubic * u * u * u))
+            hidden[b, tile_rows(i), :] = (0.5 * u * (1.0 + tangent)).astype(bf16)
+            slope[b, tile_rows(i), :] = 0.5 * (1.0 + tangent) + 0.5 * u * (1.0 - tangent * tangent) * gelu_scale * (
+                1.0 + 3.0 * gelu_cubic * u * u
+            )
+
+    relay(1, 1)
+    gathered(1, 0)
+    gathered(1, 1)
+    nt = (((1,), (1,)), ((), ()))
+    split = features // 2
+
+    def project(r, h):
+        value = 0.0
+        for b in range(2):
+            value = value + lax.dot_general(
+                hidden[b, half(r), :], second[b, pl.ds(h * split, split), :], nt, preferred_element_type=f32
+            )
+        return value
+
+    for h in range(2):
+        part_out[h] = project(1, h).astype(bf16)
+        send(part_out.at[h], part_in.at[h], ps.at[h], pr.at[h], pair)
+    for h in range(2):
+        unit[:, pl.ds(h * split, split)] = project(0, h)
+
+    for k in range(1, replicas):
+        origin = (d + replicas - k) % replicas
+        arrive(
+            coming.at[pl.ds(pl.multiple_of(origin * slot_rows, slot_rows), slot_rows)], ur.at[k], us.at[k]
+        )
+    picker = jnp.where(slot_col == lanes, 1.0, 0.0).astype(bf16)
+    cot[...] = jnp.dot(picker, coming[...], preferred_element_type=f32)
+    for h in range(2):
+        arrive(part_in.at[h], pr.at[h], ps.at[h])
+
+    @pl.loop(0, share // TILE)
+    def _(i):
+        rows = tile_rows(i)
+        partner = jnp.concatenate([part_in[h, rows, :].astype(f32) for h in range(2)], axis=1)
+        residual = rows_in[rows, :].astype(f32) + (unit[rows, :] + partner)
+        unit_out, scale_out = normalize(residual)
+        merged[rows, :] = (unit_out * merge_gain[...] + merge_bias[...]).astype(bf16)
+        grad_rows[rows, :] = norm_backward(cot[rows, :], unit_out, scale_out, merge_gain[...]).astype(bf16)
+
+    send(grad_rows.at[half(0)], grad_rows.at[half(1)], xs.at[0], xr.at[0], pair)
+
+    picker_t = jnp.where(subs == slot_row, 1.0, 0.0).astype(bf16)
+    outgoing[...] = jnp.dot(picker_t, merged[...], preferred_element_type=f32).astype(bf16)
+    own_slots = pl.ds(pl.multiple_of(d * slot_rows, slot_rows), slot_rows)
+    keep = pltpu.make_async_copy(outgoing.at[own_slots], received.at[own_slots], local_sem.at[5])
+    keep.start()
+    for k in range(1, replicas):
+        peer = (d + k) % replicas
+        send(
+            outgoing.at[pl.ds(pl.multiple_of(peer * slot_rows, slot_rows), slot_rows)],
+            received.at[own_slots],
+            os_.at[k],
+            or_.at[k],
+            (s, peer),
+        )
+
+    def back(r):
+        for b in range(2):
+            grad_hidden = jnp.dot(grad_rows[half(r), :], second[b], preferred_element_type=f32)
+            grad_pre[b, half(r), :] = (grad_hidden * slope[b, half(r), :]).astype(bf16)
+
+    flip(grad_rows, grad_rows_t, 0)
+    back(0)
+    arrive(grad_rows.at[half(1)], xr.at[0], xs.at[0])
+    flip(grad_rows, grad_rows_t, 1)
+
+    order = list(range(1, chips)) + [0]
+
+    def scatter(w, lhs, rhs):
+        def piece(j, b):
+            return jnp.dot(lhs[shard_rows(j), :], rhs[b], preferred_element_type=f32)
+
+        for k in order:
+            for b in range(2):
+                core_out[w, k, b] = piece(chip_at(k) * 2 + mate_core, b).astype(bf16)
+            send(core_out.at[w, k], core_in.at[w, k], cs.at[w, k], cr.at[w, k], mate)
+        for k in order:
+            arrive(core_in.at[w, k], cr.at[w, k], cs.at[w, k])
+            for b in range(2):
+                value = piece(chip_at(k) * 2 + c, b) + core_in[w, k, b].astype(f32)
+                if k:
+                    chip_out[w, k, b] = value.astype(bf16)
+                else:
+                    total[w, b] = value
+            if k:
+                send(chip_out.at[w, k], chip_in.at[w, k], hs.at[w, k], hr.at[w, k], (s, chip_at(k) * 2 + c))
+
+    def collect(w):
+        for k in range(1, chips):
+            arrive(chip_in.at[w, k], hr.at[w, k], hs.at[w, k])
+        for b in (1, 0):
+            value = total[w, b]
+            for k in range(1, chips):
+                value = value + chip_in[w, k, b].astype(f32)
+            if b:
+                cross_out[w] = value.astype(bf16)
+                send(cross_out.at[w], cross_in.at[w], zs.at[w], zr.at[w], across)
+            else:
+                total[w, 0] = value
+
+    def finish(w, out):
+        arrive(cross_in.at[w], zr.at[w], zs.at[w])
+        out[...] = total[w, 0] + cross_in[w].astype(f32)
+
+    scatter(1, grad_rows_t, hidden)
+    back(1)
+    scatter(0, normed_t, grad_pre)
+    collect(1)
+    keep.wait()
+    for k in range(1, replicas):
+        origin = (d + replicas - k) % replicas
+        arrive(
+            received.at[pl.ds(pl.multiple_of(origin * slot_rows, slot_rows), slot_rows)], or_.at[k], os_.at[k]
+        )
+    finish(1, grad_out)
+    collect(0)
+    finish(0, grad_in)
+    for copy in sent:
+        copy.wait_send()
+
+
+def in_one_kernel(patches, pre_gain, merge_gain, merge_bias, w_in, w_out, destinations, upstream):
+    sections = lax.axis_size("section")
+    replicas = lax.axis_size("dp")
+    chips = replicas // 2
+    share = patches.shape[0] // sections
+    features = patches.shape[1]
+    merge = upstream.shape[1] // features
+    blocks, width = destinations.shape[0], w_in.shape[1]
+    shard = w_in.shape[0]
+    capacity = upstream.shape[0] // replicas
+    f32, bf16 = jnp.float32, jnp.bfloat16
+    targets = jnp.repeat(destinations[:, 0], merge).astype(f32)
+    block_ids = np.repeat(np.arange(blocks), merge).astype(np.float32)
+    member = np.tile(np.arange(merge), blocks).astype(np.float32)
+    vmem = pl.BlockSpec(memory_space=pltpu.VMEM)
+    hbm = pl.BlockSpec(memory_space=pl.ANY)
+    dma = pltpu.SemaphoreType.DMA
+    received, grad_in, grad_out_t = pl.pallas_call(
+        functools.partial(window_kernel, sections, replicas, merge, capacity),
+        out_shape=(
+            jax.ShapeDtypeStruct((upstream.shape[0] * merge, features), bf16),
+            jax.ShapeDtypeStruct((shard, width), f32),
+            jax.ShapeDtypeStruct((shard, width), f32),
+        ),
+        in_specs=[hbm, vmem, vmem, vmem, hbm, hbm] + [vmem] * 6 + [hbm],
+        out_specs=(hbm, vmem, vmem),
+        scratch_shapes=[
+            pltpu.VMEM((2 * share, features), bf16),
+            pltpu.VMEM((2 * share, features), bf16),
+            pltpu.VMEM((features, 2 * share), bf16),
+            pltpu.VMEM((2, features, width), bf16),
+            pltpu.VMEM((2, features, width), bf16),
+            pltpu.VMEM((2, 2 * share, width), f32),
+            pltpu.VMEM((2, 2 * share, width), bf16),
+            pltpu.VMEM((2, share, features // 2), bf16),
+            pltpu.VMEM((2, share, features // 2), bf16),
+            pltpu.VMEM((share, features), f32),
+            pltpu.VMEM((8, 128), f32),
+            pltpu.VMEM((share, features), bf16),
+            pltpu.VMEM((share, features), bf16),
+            pltpu.VMEM((share, features), bf16),
+            pltpu.VMEM((share, features), f32),
+            pltpu.VMEM((2 * share, features), bf16),
+            pltpu.VMEM((features, 2 * share), bf16),
+            pltpu.VMEM((2, 2 * share, width), bf16),
+            pltpu.VMEM((2, chips, 2, shard, width), bf16),
+            pltpu.VMEM((2, chips, 2, shard, width), bf16),
+            pltpu.VMEM((2, chips, 2, shard, width), bf16),
+            pltpu.VMEM((2, chips, 2, shard, width), bf16),
+            pltpu.VMEM((2, 2, shard, width), f32),
+            pltpu.VMEM((2, shard, width), bf16),
+            pltpu.VMEM((2, shard, width), bf16),
+            dma((6,)),
+            dma((2, 2, 2 * chips)),
+            dma((2, 2, 2 * chips)),
+            dma((replicas,)),
+            dma((replicas,)),
+            dma((replicas,)),
+            dma((replicas,)),
+            dma((2,)),
+            dma((2,)),
+            dma((1,)),
+            dma((1,)),
+            dma((2, chips)),
+            dma((2, chips)),
+            dma((2, chips)),
+            dma((2, chips)),
+            dma((2,)),
+            dma((2,)),
+        ],
+        compiler_params=pltpu.CompilerParams(
+            collective_id=0, has_side_effects=True, vmem_limit_bytes=60 * 1024 * 1024
+        ),
+    )(
+        patches,
+        pre_gain[None, :],
+        merge_gain[None, :],
+        merge_bias[None, :],
+        w_in,
+        w_out.T,
+        targets[:, None],
+        targets[None, :],
+        block_ids[:, None],
+        block_ids[None, :],
+        member[:, None],
+        member[None, :],
+        upstream.reshape(-1, features),
+    )
+    return (received.reshape(upstream.shape), grad_in, grad_out_t.T)
+
+
+def window(*args):
+    patches, w_in, upstream = args[0], args[4], args[7]
+    sections = lax.axis_size("section")
+    replicas = lax.axis_size("dp")
+    share = patches.shape[0] // sections
+    slots = upstream.shape[0] * upstream.shape[1] // patches.shape[1]
+    aligned = w_in.shape[0] % 16 == 0 and w_in.shape[1] % 128 == 0 and patches.shape[1] % 256 == 0
+    if aligned and sections == 4 and replicas % 2 == 0 and slots == share:
+        return in_one_kernel(*args)
+    return on_device(*args)
+
+
 def solution(mesh):
     return jax.shard_map(
-        on_device,
+        window,
         mesh=mesh,
         in_specs=(
             P("dp", None),

time: 285 us -> 150 us (0.53)
  waiting for transfers between devices: 170 us -> 0 us
  Pallas kernels: 0 us -> 135 us
  other arithmetic: 32.7 us -> 0.66 us
  matrix products: 30.6 us -> 0 us
  blocking collectives: 19 us -> 0 us
  between operations: 14.3 us -> 0.64 us
  starting transfers between devices: 4.18 us -> 0 us
    pallas_call x0 -> x1, Pallas kernels: none -> 135 us  [in_one_kernel(): pl.pallas_call(functools.partial(window_kernel, sections, replicas, merge...]
    all_gather x3 -> x0, waiting for transfers between devices: 104 us -> none  [the longest x1 54.4 us: on_device(): grad_residual = lax.all_gather(grad_own, 'section', axis=0, tiled=True)]
    reduce_scatter x3 -> x0, waiting for transfers between devices: 56.9 us -> none  [the longest x1 40.1 us: on_device(): lax.psum_scatter(grad_second.astype(jnp.bfloat16), 'dp', scatter_dimensio...]
    dot_general x6 -> x0, matrix products: 30.6 us -> none  [the longest x1 9.76 us: on_device(): lax.dot_general(normed, grad_preact, (((0,), (0,)), ((), ())), preferred_...]
    all_to_all x4 -> x0, other arithmetic: 19.6 us -> none  [the longest x2 11 us: on_device(): lax.all_to_all(upstream.reshape(replicas, capacity * block_width), 'dp',...]
    all_to_all x1 -> x0, blocking collectives: 19 us -> none  [on_device(): lax.all_to_all(outgoing.reshape(replicas, capacity * block_width), 'dp',...]
    all_to_all x1 -> x0, waiting for transfers between devices: 7.92 us -> none  [on_device(): lax.all_to_all(upstream.reshape(replicas, capacity * block_width), 'dp',...]
    convert_element_type x4 -> x1, other arithmetic: 7.48 us -> 0.66 us  [in_one_kernel(): targets = jnp.repeat(destinations[:, 0], merge).astype(f32)]
  transfers between devices with their start and end apart: 7 -> 0, of which waited for: 7 -> 0; matrix products, arithmetic and copies ran while one was open for 18% -> 0% of each run, Pallas kernels for 0% -> 0%
where the time goes in v2:
time: 150 us
  Pallas kernels  135 us (90%)
  local copies, waits for them, and re-layouts  13.4 us (9%)
    pallas_call x1, Pallas kernels, in_one_kernel(): pl.pallas_call(functools.partial(window_kernel, sections, replicas, merge...  135 us
    unnamed x2, local copies, waits for them, and re-layouts  3.56 us

profile of v2, /device:TPU:0, one launch (start us, length us, event | category | flops | bytes accessed | tf_op | source)
XLA Modules:
  0.0 149.8 jit_solution(5917657785217263379)
XLA Ops:
  0.6 0.7 convert_bitcast_fusion
  1.3 1.3 broadcast_in_dim.14.pre_gain
  2.6 1.3 broadcast_in_dim.15.merge_gain
  3.9 1.3 broadcast_in_dim.16.merge_bias
  5.2 0.1 broadcast_in_dim.17
  5.2 0.7 convert_element_type.32.trow
  5.9 0.7 convert_element_type.33.tcol
  6.7 2.2 %reshape.37.upstream = bf16[256,1280]{1,0:T(8,128)(2,1)} reshape(bf16[64,5120]{1,0:T(8,128)(2,1)} %param.19) | data formatting | bytes 1310720 | tf_op jit(solution)/shard_map/reshape | solution.py:502
  8.9 135.1 %shard_map.139 = (bf16[256,1280]{1,0:T(8,128)(2,1)}, f32[160,640]{1,0:T(8,128)}, f32[160,640]{1,0:T(8,128)}) custom-call(bf16[1024,1280]{1,0:T(8,128)(2,1)} %patches.1, f32[1,1280]{1,0:T(1,128)} %broadcast_in_dim.14.pre_gain, f32[1,1280]{1,0:T(1,128)} %broadcast_in_dim.15.merge_gain, f32[1,1280]{1,0:T(1,128)} %broadcast_in_dim.16.merge_bias, ...), custom_call_target="tpu_custom_call" | custom-call | tf_op jit(solution)/shard_map/pallas_call | solution.py:433
  144.0 2.2 %reshape.38 = bf16[64,5120]{1,0:T(8,128)(2,1)} reshape(bf16[256,1280]{1,0:T(8,128)(2,1)} %get-tuple-element.6) | data formatting | bytes 1310720 | tf_op jit(solution)/shard_map/reshape | solution.py:504
  146.3 1.8 %copy.18 = f32[160,640]{1,0:T(8,128)} copy(f32[160,640]{1,0:T(8,128)} %get-tuple-element.13) | data formatting | bytes 819200
  148.0 1.8 %copy.19 = f32[640,160]{0,1:T(8,128)} copy(f32[640,160]{0,1:T(8,128)} %bitcast.4) | data formatting | bytes 819200

commit v3 on v2

--- a/solution.py
+++ b/solution.py
@@ -157,8 +157,11 @@
     mate_core = 1 - c
     mate = (s, q * 2 + mate_core)
 
-    def chip_at(k):
-        return (q + k) % chips
+    beside, below = q + 1 - 2 * (q % 2), (q + 2) % chips
+    corner = (beside + 2) % chips
+
+    def side(b):
+        return (below, beside) if b == 0 else (beside, below)
 
     def shard_rows(j):
         return pl.ds(pl.multiple_of(j * shard, 16), shard)
@@ -211,28 +214,60 @@
 
     def spread(w, b):
         src = shards[w] if b == 0 else fulls[w].at[1, shard_rows(d)]
-        for k in range(1, chips):
-            send(src, fulls[w].at[b, shard_rows(d)], gs.at[w, b, 1 + k], gr.at[w, b, 1 + k], (s, chip_at(k) * 2 + c))
-        send(src, fulls[w].at[b, shard_rows(d)], gs.at[w, b, 1], gr.at[w, b, 1], mate)
-
-    def relay(w, b):
-        for k in range(1, chips):
-            place = fulls[w].at[b, shard_rows(chip_at(chips - k) * 2 + c)]
-            arrive(place, gr.at[w, b, 1 + k], gs.at[w, b, 1 + k])
-            send(place, place, gs.at[w, b, chips + k], gr.at[w, b, chips + k], mate)
-
-    def gathered(w, b):
-        arrive(fulls[w].at[b, shard_rows(q * 2 + mate_core)], gr.at[w, b, 1], gs.at[w, b, 1])
-        for k in range(1, chips):
-            place = fulls[w].at[b, shard_rows(chip_at(chips - k) * 2 + mate_core)]
-            arrive(place, gr.at[w, b, chips + k], gs.at[w, b, chips + k])
+        place = fulls[w].at[b, shard_rows(d)]
+        peers = [(s, chip * 2 + c) for chip in side(b)] + [mate]
+        for slot, peer in enumerate(peers, 1):
+            send(src, place, gs.at[w, b, slot], gr.at[w, b, slot], peer)
+
+    def origin_of(b, slot):
+        return {1: side(b)[0], 2: side(b)[1], 4: corner}[slot]
+
+    def got(w, b, slot):
+        place = fulls[w].at[b, shard_rows(origin_of(b, slot) * 2 + c)]
+        arrive(place, gr.at[w, b, slot], gs.at[w, b, slot])
+        if slot == 1:
+            send(place, place, gs.at[w, b, 4], gr.at[w, b, 4], (s, side(b)[1] * 2 + c))
+        to_mate = {1: 5, 2: 6, 4: 7}[slot]
+        send(place, place, gs.at[w, b, to_mate], gr.at[w, b, to_mate], mate)
+
+    def from_mate(w, b, slot):
+        chip = q if slot == 3 else origin_of(b, {5: 1, 6: 2, 7: 4}[slot])
+        arrive(fulls[w].at[b, shard_rows(chip * 2 + mate_core)], gr.at[w, b, slot], gs.at[w, b, slot])
 
     spread(0, 0)
     arrive(first.at[1, shard_rows(d)], gr.at[0, 1, 0], gs.at[0, 1, 0])
     spread(0, 1)
+    got(0, 0, 1)
     spread(1, 0)
+    got(0, 1, 1)
     arrive(second.at[1, shard_rows(d)], gr.at[1, 1, 0], gs.at[1, 1, 0])
     spread(1, 1)
+
+    for copy in loads:
+        copy.wait()
+
+    def tile_rows(i):
+        return pl.ds(pl.multiple_of(i * TILE, TILE), TILE)
+
+    @pl.loop(0, 2 * share // TILE)
+    def _(i):
+        unit_rows, _ = normalize(rows_in[tile_rows(i), :].astype(f32))
+        normed[tile_rows(i), :] = (unit_rows * pre_gain[...][None, :]).astype(bf16)
+
+    def flip(src, dst, r):
+        @pl.loop(0, features // 128)
+        def _(i):
+            cols = pl.ds(pl.multiple_of(i * 128, 128), 128)
+            dst[cols, pl.ds(r * share, share)] = src[pl.ds(r * share, share), cols].T
+
+    got(0, 0, 2)
+    got(0, 1, 2)
+    got(1, 0, 1)
+    flip(normed, normed_t, 0)
+    got(0, 0, 4)
+    got(0, 1, 4)
+    flip(normed, normed_t, 1)
+    got(1, 1, 1)
     for k in range(1, replicas):
         peer = (d + k) % replicas
         send(
@@ -243,28 +278,6 @@
             (s, peer),
         )
 
-    for copy in loads:
-        copy.wait()
-
-    def tile_rows(i):
-        return pl.ds(pl.multiple_of(i * TILE, TILE), TILE)
-
-    @pl.loop(0, 2 * share // TILE)
-    def _(i):
-        unit_rows, _ = normalize(rows_in[tile_rows(i), :].astype(f32))
-        normed[tile_rows(i), :] = (unit_rows * pre_gain[...]).astype(bf16)
-
-    def flip(src, dst, r):
-        @pl.loop(0, features // 128)
-        def _(i):
-            cols = pl.ds(pl.multiple_of(i * 128, 128), 128)
-            dst[cols, pl.ds(r * share, share)] = src[pl.ds(r * share, share), cols].T
-
-    relay(0, 0)
-    flip(normed, normed_t, 0)
-    flip(normed, normed_t, 1)
-    relay(0, 1)
-
     matches = tcol[...] == trow[...]
     above = jnp.where(matches & (brow[...] < bcol[...]) & (mrow[...] == 0.0), 1.0, 0.0)
     left = jnp.where(matches & (bcol[...] < brow[...]) & (mcol[...] == 0.0), 1.0, 0.0)
@@ -277,11 +290,13 @@
         return pl.ds(r * share, share)
 
     for b in range(2):
-        gathered(0, b)
+        for slot in (3, 5, 6, 7):
+            from_mate(0, b, slot)
         for r in range(2):
             slope[b, half(r), :] = jnp.dot(normed[half(r), :], first[b], preferred_element_type=f32)
         if b == 0:
-            relay(1, 0)
+            got(1, 0, 2)
+            got(1, 1, 2)
 
         @pl.loop(0, 2 * share // TILE)
         def _(i):
@@ -292,9 +307,6 @@
                 1.0 + 3.0 * gelu_cubic * u * u
             )
 
-    relay(1, 1)
-    gathered(1, 0)
-    gathered(1, 1)
     nt = (((1,), (1,)), ((), ()))
     split = features // 2
 
@@ -302,13 +314,25 @@
         value = 0.0
         for b in range(2):
             value = value + lax.dot_general(
-                hidden[b, half(r), :], second[b, pl.ds(h * split, split), :], nt, preferred_element_type=f32
+                hidden[b, half(r), :],
+                second[b, pl.ds(pl.multiple_of(h * split, 128), split), :],
+                nt,
+                preferred_element_type=f32,
             )
         return value
 
-    for h in range(2):
+    near = q // 2
+    for step, h in enumerate((near, 1 - near)):
+        if step == 0:
+            for b, slot in ((0, 3), (1, 3), (0, 6), (1, 5)):
+                from_mate(1, b, slot)
+        else:
+            got(1, 0, 4)
+            got(1, 1, 4)
+            for b, slot in ((0, 5), (1, 6), (0, 7), (1, 7)):
+                from_mate(1, b, slot)
         part_out[h] = project(1, h).astype(bf16)
-        send(part_out.at[h], part_in.at[h], ps.at[h], pr.at[h], pair)
+        send(part_out.at[h], part_in.at[h], ps.at[step], pr.at[step], pair)
     for h in range(2):
         unit[:, pl.ds(h * split, split)] = project(0, h)
 
@@ -319,8 +343,8 @@
         )
     picker = jnp.where(slot_col == lanes, 1.0, 0.0).astype(bf16)
     cot[...] = jnp.dot(picker, coming[...], preferred_element_type=f32)
-    for h in range(2):
-        arrive(part_in.at[h], pr.at[h], ps.at[h])
+    for step, h in enumerate((near, 1 - near)):
+        arrive(part_in.at[h], pr.at[step], ps.at[step])
 
     @pl.loop(0, share // TILE)
     def _(i):
@@ -328,8 +352,8 @@
         partner = jnp.concatenate([part_in[h, rows, :].astype(f32) for h in range(2)], axis=1)
         residual = rows_in[rows, :].astype(f32) + (unit[rows, :] + partner)
         unit_out, scale_out = normalize(residual)
-        merged[rows, :] = (unit_out * merge_gain[...] + merge_bias[...]).astype(bf16)
-        grad_rows[rows, :] = norm_backward(cot[rows, :], unit_out, scale_out, merge_gain[...]).astype(bf16)
+        merged[rows, :] = (unit_out * merge_gain[...][None, :] + merge_bias[...][None, :]).astype(bf16)
+        grad_rows[rows, :] = norm_backward(cot[rows, :], unit_out, scale_out, merge_gain[...][None, :]).astype(bf16)
 
     send(grad_rows.at[half(0)], grad_rows.at[half(1)], xs.at[0], xr.at[0], pair)
 
@@ -358,48 +382,62 @@
     arrive(grad_rows.at[half(1)], xr.at[0], xs.at[0])
     flip(grad_rows, grad_rows_t, 1)
 
-    order = list(range(1, chips)) + [0]
-
-    def scatter(w, lhs, rhs):
-        def piece(j, b):
-            return jnp.dot(lhs[shard_rows(j), :], rhs[b], preferred_element_type=f32)
-
-        for k in order:
-            for b in range(2):
-                core_out[w, k, b] = piece(chip_at(k) * 2 + mate_core, b).astype(bf16)
-            send(core_out.at[w, k], core_in.at[w, k], cs.at[w, k], cr.at[w, k], mate)
-        for k in order:
-            arrive(core_in.at[w, k], cr.at[w, k], cs.at[w, k])
-            for b in range(2):
-                value = piece(chip_at(k) * 2 + c, b) + core_in[w, k, b].astype(f32)
-                if k:
-                    chip_out[w, k, b] = value.astype(bf16)
-                else:
-                    total[w, b] = value
-            if k:
-                send(chip_out.at[w, k], chip_in.at[w, k], hs.at[w, k], hr.at[w, k], (s, chip_at(k) * 2 + c))
-
-    def collect(w):
-        for k in range(1, chips):
-            arrive(chip_in.at[w, k], hr.at[w, k], hs.at[w, k])
-        for b in (1, 0):
-            value = total[w, b]
-            for k in range(1, chips):
-                value = value + chip_in[w, k, b].astype(f32)
-            if b:
-                cross_out[w] = value.astype(bf16)
-                send(cross_out.at[w], cross_in.at[w], zs.at[w], zr.at[w], across)
-            else:
-                total[w, 0] = value
+    def piece(w, j, b):
+        lhs, rhs = ((normed_t, grad_pre), (grad_rows_t, hidden))[w]
+        return jnp.dot(lhs[shard_rows(j), :], rhs[b], preferred_element_type=f32)
+
+    def both_cores(w, b, k, chip):
+        value = piece(w, chip * 2 + c, b)
+        arrive(core_in.at[w, b, k], cr.at[w, b, k], cs.at[w, b, k])
+        return value + core_in[w, b, k].astype(f32)
+
+    def pass_on(w, b, k, value, chip):
+        chip_out[w, b, k] = value.astype(bf16)
+        send(chip_out.at[w, b, k], chip_in.at[w, b, k], hs.at[w, b, k], hr.at[w, b, k], (s, chip * 2 + c))
+
+    def taken(w, b, k):
+        arrive(chip_in.at[w, b, k], hr.at[w, b, k], hs.at[w, b, k])
+        return chip_in[w, b, k].astype(f32)
+
+    def begin(w, b):
+        lead, follow = side(b)
+        for k, chip in enumerate((corner, lead, follow, q)):
+            core_out[w, b, k] = piece(w, chip * 2 + mate_core, b).astype(bf16)
+            send(core_out.at[w, b, k], core_in.at[w, b, k], cs.at[w, b, k], cr.at[w, b, k], mate)
+        pass_on(w, b, 0, both_cores(w, b, 0, corner), lead)
+        pass_on(w, b, 1, both_cores(w, b, 1, lead), lead)
+
+    def middle(w, b):
+        follow = side(b)[1]
+        value = both_cores(w, b, 2, follow)
+        pass_on(w, b, 2, value + taken(w, b, 0), follow)
+        total[w, b] = both_cores(w, b, 3, q)
+
+    def close(w, b):
+        value = total[w, b] + taken(w, b, 1)
+        value = value + taken(w, b, 2)
+        if b:
+            cross_out[w] = value.astype(bf16)
+            send(cross_out.at[w], cross_in.at[w], zs.at[w], zr.at[w], across)
+        else:
+            total[w, 0] = value
 
     def finish(w, out):
         arrive(cross_in.at[w], zr.at[w], zs.at[w])
         out[...] = total[w, 0] + cross_in[w].astype(f32)
 
-    scatter(1, grad_rows_t, hidden)
+    begin(1, 1)
+    begin(1, 0)
     back(1)
-    scatter(0, normed_t, grad_pre)
-    collect(1)
+    middle(1, 1)
+    begin(0, 1)
+    middle(1, 0)
+    begin(0, 0)
+    close(1, 1)
+    middle(0, 1)
+    close(1, 0)
+    middle(0, 0)
+    close(0, 1)
     keep.wait()
     for k in range(1, replicas):
         origin = (d + replicas - k) % replicas
@@ -407,7 +445,7 @@
             received.at[pl.ds(pl.multiple_of(origin * slot_rows, slot_rows), slot_rows)], or_.at[k], os_.at[k]
         )
     finish(1, grad_out)
-    collect(0)
+    close(0, 0)
     finish(0, grad_in)
     for copy in sent:
         copy.wait_send()
@@ -458,10 +496,10 @@
             pltpu.VMEM((2 * share, features), bf16),
             pltpu.VMEM((features, 2 * share), bf16),
             pltpu.VMEM((2, 2 * share, width), bf16),
-            pltpu.VMEM((2, chips, 2, shard, width), bf16),
-            pltpu.VMEM((2, chips, 2, shard, width), bf16),
-            pltpu.VMEM((2, chips, 2, shard, width), bf16),
-            pltpu.VMEM((2, chips, 2, shard, width), bf16),
+            pltpu.VMEM((2, 2, chips, shard, width), bf16),
+            pltpu.VMEM((2, 2, chips, shard, width), bf16),
+            pltpu.VMEM((2, 2, chips - 1, shard, width), bf16),
+            pltpu.VMEM((2, 2, chips - 1, shard, width), bf16),
             pltpu.VMEM((2, 2, shard, width), f32),
             pltpu.VMEM((2, shard, width), bf16),
             pltpu.VMEM((2, shard, width), bf16),
@@ -476,10 +514,10 @@
             dma((2,)),
             dma((1,)),
             dma((1,)),
-            dma((2, chips)),
-            dma((2, chips)),
-            dma((2, chips)),
-            dma((2, chips)),
+            dma((2, 2, chips)),
+            dma((2, 2, chips)),
+            dma((2, 2, chips - 1)),
+            dma((2, 2, chips - 1)),
             dma((2,)),
             dma((2,)),
         ],
@@ -488,9 +526,9 @@
         ),
     )(
         patches,
-        pre_gain[None, :],
-        merge_gain[None, :],
-        merge_bias[None, :],
+        pre_gain,
+        merge_gain,
+        merge_bias,
         w_in,
         w_out.T,
         targets[:, None],
@@ -511,7 +549,7 @@
     share = patches.shape[0] // sections
     slots = upstream.shape[0] * upstream.shape[1] // patches.shape[1]
     aligned = w_in.shape[0] % 16 == 0 and w_in.shape[1] % 128 == 0 and patches.shape[1] % 256 == 0
-    if aligned and sections == 4 and replicas % 2 == 0 and slots == share:
+    if aligned and sections == 4 and replicas == 8 and slots == share:
         return in_one_kernel(*args)
     return on_device(*args)
 

time: 150 us -> 131 us (0.87)
  Pallas kernels: 135 us -> 120 us
  local copies, waits for them, and re-layouts: 13.4 us -> 9.54 us
    pallas_call x1, Pallas kernels: 135 us -> 120 us  [in_one_kernel(): pl.pallas_call(functools.partial(window_kernel, sections, replicas, merge...]
    broadcast_in_dim x3 -> x0, local copies, waits for them, and re-layouts: 3.87 us -> none  [the longest x1 1.29 us: in_one_kernel(): pre_gain[None, :]]
where the time goes in v3:
time: 131 us
  Pallas kernels  120 us (92%)
  local copies, waits for them, and re-layouts  9.54 us (7%)
    pallas_call x1, Pallas kernels, in_one_kernel(): pl.pallas_call(functools.partial(window_kernel, sections, replicas, merge...  120 us
    unnamed x2, local copies, waits for them, and re-layouts  3.56 us

profile of v3, /device:TPU:0, one launch (start us, length us, event | category | flops | bytes accessed | tf_op | source)
XLA Modules:
  0.0 130.7 jit_solution(7079590963921126950)
XLA Ops:
  0.6 0.7 convert_bitcast_fusion
  1.3 0.1 broadcast_in_dim.2
  1.4 0.7 convert_element_type.32.trow
  2.0 0.7 convert_element_type.33.tcol
  2.8 2.2 %reshape.37.upstream = bf16[256,1280]{1,0:T(8,128)(2,1)} reshape(bf16[64,5120]{1,0:T(8,128)(2,1)} %param.19) | data formatting | bytes 1310720 | tf_op jit(solution)/shard_map/reshape | solution.py:540
  5.0 119.8 %shard_map.139 = (bf16[256,1280]{1,0:T(8,128)(2,1)}, f32[160,640]{1,0:T(8,128)}, f32[160,640]{1,0:T(8,128)}) custom-call(bf16[1024,1280]{1,0:T(8,128)(2,1)} %patches.1, f32[1280]{0:T(1024)} %pre_gain.1, f32[1280]{0:T(1024)} %merge_gain.1, f32[1280]{0:T(1024)} %merge_bias.1, bf16[160,640]{1,0:T(8,128)(2,1)} %w_in.1, bf16[160,640]{1,0:T(8,128)(2,1)} %bitcast.5, ...), custom_call_target="tpu_custom_call" | custom-call | tf_op jit(solution)/shard_map/pallas_call | solution.py:471
  124.9 2.2 %reshape.38 = bf16[64,5120]{1,0:T(8,128)(2,1)} reshape(bf16[256,1280]{1,0:T(8,128)(2,1)} %get-tuple-element.6) | data formatting | bytes 1310720 | tf_op jit(solution)/shard_map/reshape | solution.py:542
  127.1 1.8 %copy.18 = f32[160,640]{1,0:T(8,128)} copy(f32[160,640]{1,0:T(8,128)} %get-tuple-element.13) | data formatting | bytes 819200
  128.9 1.8 %copy.19 = f32[640,160]{0,1:T(8,128)} copy(f32[640,160]{0,1:T(8,128)} %bitcast.4) | data formatting | bytes 819200

commit v4 on v3

--- a/solution.py
+++ b/solution.py
@@ -160,8 +160,8 @@
     beside, below = q + 1 - 2 * (q % 2), (q + 2) % chips
     corner = (beside + 2) % chips
 
-    def side(b):
-        return (below, beside) if b == 0 else (beside, below)
+    def side(w, b):
+        return (below, beside) if w == b else (beside, below)
 
     def shard_rows(j):
         return pl.ds(pl.multiple_of(j * shard, 16), shard)
@@ -215,31 +215,31 @@
     def spread(w, b):
         src = shards[w] if b == 0 else fulls[w].at[1, shard_rows(d)]
         place = fulls[w].at[b, shard_rows(d)]
-        peers = [(s, chip * 2 + c) for chip in side(b)] + [mate]
+        peers = [(s, chip * 2 + c) for chip in side(w, b)] + [mate]
         for slot, peer in enumerate(peers, 1):
             send(src, place, gs.at[w, b, slot], gr.at[w, b, slot], peer)
 
-    def origin_of(b, slot):
-        return {1: side(b)[0], 2: side(b)[1], 4: corner}[slot]
+    def origin_of(w, b, slot):
+        return {1: side(w, b)[0], 2: side(w, b)[1], 4: corner}[slot]
 
     def got(w, b, slot):
-        place = fulls[w].at[b, shard_rows(origin_of(b, slot) * 2 + c)]
+        place = fulls[w].at[b, shard_rows(origin_of(w, b, slot) * 2 + c)]
         arrive(place, gr.at[w, b, slot], gs.at[w, b, slot])
         if slot == 1:
-            send(place, place, gs.at[w, b, 4], gr.at[w, b, 4], (s, side(b)[1] * 2 + c))
+            send(place, place, gs.at[w, b, 4], gr.at[w, b, 4], (s, side(w, b)[1] * 2 + c))
         to_mate = {1: 5, 2: 6, 4: 7}[slot]
         send(place, place, gs.at[w, b, to_mate], gr.at[w, b, to_mate], mate)
 
     def from_mate(w, b, slot):
-        chip = q if slot == 3 else origin_of(b, {5: 1, 6: 2, 7: 4}[slot])
+        chip = q if slot == 3 else origin_of(w, b, {5: 1, 6: 2, 7: 4}[slot])
         arrive(fulls[w].at[b, shard_rows(chip * 2 + mate_core)], gr.at[w, b, slot], gs.at[w, b, slot])
 
     spread(0, 0)
+    spread(1, 0)
+    got(0, 0, 1)
+    got(1, 0, 1)
     arrive(first.at[1, shard_rows(d)], gr.at[0, 1, 0], gs.at[0, 1, 0])
     spread(0, 1)
-    got(0, 0, 1)
-    spread(1, 0)
-    got(0, 1, 1)
     arrive(second.at[1, shard_rows(d)], gr.at[1, 1, 0], gs.at[1, 1, 0])
     spread(1, 1)
 
@@ -261,13 +261,11 @@
             dst[cols, pl.ds(r * share, share)] = src[pl.ds(r * share, share), cols].T
 
     got(0, 0, 2)
-    got(0, 1, 2)
-    got(1, 0, 1)
+    got(0, 0, 4)
+    got(0, 1, 1)
+    got(1, 1, 1)
     flip(normed, normed_t, 0)
-    got(0, 0, 4)
-    got(0, 1, 4)
     flip(normed, normed_t, 1)
-    got(1, 1, 1)
     for k in range(1, replicas):
         peer = (d + k) % replicas
         send(
@@ -290,6 +288,9 @@
         return pl.ds(r * share, share)
 
     for b in range(2):
+        if b == 1:
+            got(0, 1, 2)
+            got(0, 1, 4)
         for slot in (3, 5, 6, 7):
             from_mate(0, b, slot)
         for r in range(2):
@@ -324,12 +325,12 @@
     near = q // 2
     for step, h in enumerate((near, 1 - near)):
         if step == 0:
-            for b, slot in ((0, 3), (1, 3), (0, 6), (1, 5)):
+            for b, slot in ((0, 3), (1, 3), (0, 5), (1, 6)):
                 from_mate(1, b, slot)
         else:
             got(1, 0, 4)
             got(1, 1, 4)
-            for b, slot in ((0, 5), (1, 6), (0, 7), (1, 7)):
+            for b, slot in ((0, 6), (1, 5), (0, 7), (1, 7)):
                 from_mate(1, b, slot)
         part_out[h] = project(1, h).astype(bf16)
         send(part_out.at[h], part_in.at[h], ps.at[step], pr.at[step], pair)
@@ -346,8 +347,7 @@
     for step, h in enumerate((near, 1 - near)):
         arrive(part_in.at[h], pr.at[step], ps.at[step])
 
-    @pl.loop(0, share // TILE)
-    def _(i):
+    def norm_tile(i):
         rows = tile_rows(i)
         partner = jnp.concatenate([part_in[h, rows, :].astype(f32) for h in range(2)], axis=1)
         residual = rows_in[rows, :].astype(f32) + (unit[rows, :] + partner)
@@ -355,7 +355,16 @@
         merged[rows, :] = (unit_out * merge_gain[...][None, :] + merge_bias[...][None, :]).astype(bf16)
         grad_rows[rows, :] = norm_backward(cot[rows, :], unit_out, scale_out, merge_gain[...][None, :]).astype(bf16)
 
-    send(grad_rows.at[half(0)], grad_rows.at[half(1)], xs.at[0], xr.at[0], pair)
+    tiles = share // TILE // 2
+    for step in range(2):
+        pl.loop(step * tiles, (step + 1) * tiles)(norm_tile)
+        send(
+            grad_rows.at[pl.ds(step * tiles * TILE, tiles * TILE)],
+            grad_rows.at[pl.ds(share + step * tiles * TILE, tiles * TILE)],
+            xs.at[step],
+            xr.at[step],
+            pair,
+        )
 
     picker_t = jnp.where(subs == slot_row, 1.0, 0.0).astype(bf16)
     outgoing[...] = jnp.dot(picker_t, merged[...], preferred_element_type=f32).astype(bf16)
@@ -379,7 +388,10 @@
 
     flip(grad_rows, grad_rows_t, 0)
     back(0)
-    arrive(grad_rows.at[half(1)], xr.at[0], xs.at[0])
+    for step in range(2):
+        arrive(
+            grad_rows.at[pl.ds(share + step * tiles * TILE, tiles * TILE)], xr.at[step], xs.at[step]
+        )
     flip(grad_rows, grad_rows_t, 1)
 
     def piece(w, j, b):
@@ -399,16 +411,21 @@
         arrive(chip_in.at[w, b, k], hr.at[w, b, k], hs.at[w, b, k])
         return chip_in[w, b, k].astype(f32)
 
-    def begin(w, b):
-        lead, follow = side(b)
-        for k, chip in enumerate((corner, lead, follow, q)):
+    def to_core(w, b, chosen):
+        for k in chosen:
+            chip = (corner, *side(w, b), q)[k]
             core_out[w, b, k] = piece(w, chip * 2 + mate_core, b).astype(bf16)
             send(core_out.at[w, b, k], core_in.at[w, b, k], cs.at[w, b, k], cr.at[w, b, k], mate)
+
+    def begin(w, b):
+        lead = side(w, b)[0]
+        to_core(w, b, (0, 1))
         pass_on(w, b, 0, both_cores(w, b, 0, corner), lead)
         pass_on(w, b, 1, both_cores(w, b, 1, lead), lead)
 
     def middle(w, b):
-        follow = side(b)[1]
+        follow = side(w, b)[1]
+        to_core(w, b, (2, 3))
         value = both_cores(w, b, 2, follow)
         pass_on(w, b, 2, value + taken(w, b, 0), follow)
         total[w, b] = both_cores(w, b, 3, q)
@@ -427,23 +444,23 @@
         out[...] = total[w, 0] + cross_in[w].astype(f32)
 
     begin(1, 1)
+    back(1)
+    begin(0, 1)
+    middle(1, 1)
     begin(1, 0)
-    back(1)
-    middle(1, 1)
-    begin(0, 1)
-    middle(1, 0)
+    middle(0, 1)
     begin(0, 0)
     close(1, 1)
-    middle(0, 1)
-    close(1, 0)
+    middle(1, 0)
+    close(0, 1)
     middle(0, 0)
-    close(0, 1)
     keep.wait()
     for k in range(1, replicas):
         origin = (d + replicas - k) % replicas
         arrive(
             received.at[pl.ds(pl.multiple_of(origin * slot_rows, slot_rows), slot_rows)], or_.at[k], os_.at[k]
         )
+    close(1, 0)
     finish(1, grad_out)
     close(0, 0)
     finish(0, grad_in)
@@ -512,8 +529,8 @@
             dma((replicas,)),
             dma((2,)),
             dma((2,)),
-            dma((1,)),
-            dma((1,)),
+            dma((2,)),
+            dma((2,)),
             dma((2, 2, chips)),
             dma((2, 2, chips)),
             dma((2, 2, chips - 1)),

time: 131 us -> 129 us (0.985)
  Pallas kernels: 120 us -> 117 us
    pallas_call x1, Pallas kernels: 120 us -> 117 us  [in_one_kernel(): pl.pallas_call(functools.partial(window_kernel, sections, replicas, merge...]
where the time goes in v4:
time: 129 us; the launch traced here: 128 us
  Pallas kernels  117 us (91%)
  local copies, waits for them, and re-layouts  9.54 us (7%)
    pallas_call x1, Pallas kernels, in_one_kernel(): pl.pallas_call(functools.partial(window_kernel, sections, replicas, merge...  117 us
    unnamed x2, local copies, waits for them, and re-layouts  3.56 us

profile of v4, /device:TPU:0, one launch (start us, length us, event | category | flops | bytes accessed | tf_op | source)
XLA Modules:
  0.0 128.3 jit_solution(1725195384938197516)
XLA Ops:
  0.6 0.7 convert_bitcast_fusion
  1.3 0.1 broadcast_in_dim.2
  1.4 0.7 convert_element_type.32.trow
  2.0 0.7 convert_element_type.33.tcol
  2.8 2.2 %reshape.37.upstream = bf16[256,1280]{1,0:T(8,128)(2,1)} reshape(bf16[64,5120]{1,0:T(8,128)(2,1)} %param.19) | data formatting | bytes 1310720 | tf_op jit(solution)/shard_map/reshape | solution.py:557
  5.0 117.4 %shard_map.139 = (bf16[256,1280]{1,0:T(8,128)(2,1)}, f32[160,640]{1,0:T(8,128)}, f32[160,640]{1,0:T(8,128)}) custom-call(bf16[1024,1280]{1,0:T(8,128)(2,1)} %patches.1, f32[1280]{0:T(1024)} %pre_gain.1, f32[1280]{0:T(1024)} %merge_gain.1, f32[1280]{0:T(1024)} %merge_bias.1, bf16[160,640]{1,0:T(8,128)(2,1)} %w_in.1, bf16[160,640]{1,0:T(8,128)(2,1)} %bitcast.5, ...), custom_call_target="tpu_custom_call" | custom-call | tf_op jit(solution)/shard_map/pallas_call | solution.py:488
  122.5 2.2 %reshape.38 = bf16[64,5120]{1,0:T(8,128)(2,1)} reshape(bf16[256,1280]{1,0:T(8,128)(2,1)} %get-tuple-element.6) | data formatting | bytes 1310720 | tf_op jit(solution)/shard_map/reshape | solution.py:559
  124.7 1.8 %copy.18 = f32[160,640]{1,0:T(8,128)} copy(f32[160,640]{1,0:T(8,128)} %get-tuple-element.13) | data formatting | bytes 819200
  126.5 1.8 %copy.19 = f32[640,160]{0,1:T(8,128)} copy(f32[640,160]{0,1:T(8,128)} %bitcast.4) | data formatting | bytes 819200

commit v5 on v4

--- a/solution.py
+++ b/solution.py
@@ -189,11 +189,11 @@
         pltpu.make_async_copy(w_in, first.at[0, shard_rows(d)], local_sem.at[2]),
         pltpu.make_async_copy(w_out_t, second.at[0, shard_rows(d)], local_sem.at[3]),
     ]
-    slot_rows = capacity * merge
+    slots = replicas * capacity
     loads.append(
         pltpu.make_async_copy(
-            upstream.at[pl.ds(pl.multiple_of(d * slot_rows, slot_rows), slot_rows)],
-            coming.at[pl.ds(pl.multiple_of(d * slot_rows, slot_rows), slot_rows)],
+            upstream.at[d],
+            coming.at[d],
             local_sem.at[4],
         )
     )
@@ -269,8 +269,8 @@
     for k in range(1, replicas):
         peer = (d + k) % replicas
         send(
-            upstream.at[pl.ds(pl.multiple_of(peer * slot_rows, slot_rows), slot_rows)],
-            coming.at[pl.ds(pl.multiple_of(d * slot_rows, slot_rows), slot_rows)],
+            upstream.at[peer],
+            coming.at[d],
             us.at[k],
             ur.at[k],
             (s, peer),
@@ -281,8 +281,8 @@
     left = jnp.where(matches & (bcol[...] < brow[...]) & (mcol[...] == 0.0), 1.0, 0.0)
     slot_col = (tcol[...] * capacity + jnp.sum(above, axis=1, keepdims=True)) * merge + mcol[...]
     slot_row = (trow[...] * capacity + jnp.sum(left, axis=0, keepdims=True)) * merge + mrow[...]
-    lanes = lax.broadcasted_iota(jnp.int32, (share, share), 1).astype(f32)
-    subs = lax.broadcasted_iota(jnp.int32, (share, share), 0).astype(f32)
+    lanes = lax.broadcasted_iota(jnp.int32, (share, slots), 1).astype(f32) * merge
+    subs = lax.broadcasted_iota(jnp.int32, (slots, share), 0).astype(f32) * merge
 
     def half(r):
         return pl.ds(r * share, share)
@@ -340,10 +340,14 @@
     for k in range(1, replicas):
         origin = (d + replicas - k) % replicas
         arrive(
-            coming.at[pl.ds(pl.multiple_of(origin * slot_rows, slot_rows), slot_rows)], ur.at[k], us.at[k]
-        )
-    picker = jnp.where(slot_col == lanes, 1.0, 0.0).astype(bf16)
-    cot[...] = jnp.dot(picker, coming[...], preferred_element_type=f32)
+            coming.at[origin], ur.at[k], us.at[k]
+        )
+    value = 0.0
+    for m in range(merge):
+        picker = jnp.where(slot_col == lanes + m, 1.0, 0.0).astype(bf16)
+        part = coming[:, :, pl.ds(m * features, features)].astype(f32).reshape(slots, features)
+        value = value + jnp.dot(picker, part.astype(bf16), preferred_element_type=f32)
+    cot[...] = value
     for step, h in enumerate((near, 1 - near)):
         arrive(part_in.at[h], pr.at[step], ps.at[step])
 
@@ -366,16 +370,17 @@
             pair,
         )
 
-    picker_t = jnp.where(subs == slot_row, 1.0, 0.0).astype(bf16)
-    outgoing[...] = jnp.dot(picker_t, merged[...], preferred_element_type=f32).astype(bf16)
-    own_slots = pl.ds(pl.multiple_of(d * slot_rows, slot_rows), slot_rows)
-    keep = pltpu.make_async_copy(outgoing.at[own_slots], received.at[own_slots], local_sem.at[5])
+    for m in range(merge):
+        picker_t = jnp.where(subs + m == slot_row, 1.0, 0.0).astype(bf16)
+        part = jnp.dot(picker_t, merged[...], preferred_element_type=f32)
+        outgoing[:, :, pl.ds(m * features, features)] = part.reshape(replicas, capacity, features).astype(bf16)
+    keep = pltpu.make_async_copy(outgoing.at[d], received.at[d], local_sem.at[5])
     keep.start()
     for k in range(1, replicas):
         peer = (d + k) % replicas
         send(
-            outgoing.at[pl.ds(pl.multiple_of(peer * slot_rows, slot_rows), slot_rows)],
-            received.at[own_slots],
+            outgoing.at[peer],
+            received.at[d],
             os_.at[k],
             or_.at[k],
             (s, peer),
@@ -458,7 +463,7 @@
     for k in range(1, replicas):
         origin = (d + replicas - k) % replicas
         arrive(
-            received.at[pl.ds(pl.multiple_of(origin * slot_rows, slot_rows), slot_rows)], or_.at[k], os_.at[k]
+            received.at[origin], or_.at[k], os_.at[k]
         )
     close(1, 0)
     finish(1, grad_out)
@@ -488,7 +493,7 @@
     received, grad_in, grad_out_t = pl.pallas_call(
         functools.partial(window_kernel, sections, replicas, merge, capacity),
         out_shape=(
-            jax.ShapeDtypeStruct((upstream.shape[0] * merge, features), bf16),
+            jax.ShapeDtypeStruct((replicas, capacity, upstream.shape[1]), bf16),
             jax.ShapeDtypeStruct((shard, width), f32),
             jax.ShapeDtypeStruct((shard, width), f32),
         ),
@@ -507,8 +512,8 @@
             pltpu.VMEM((share, features), f32),
             pltpu.VMEM((8, 128), f32),
             pltpu.VMEM((share, features), bf16),
-            pltpu.VMEM((share, features), bf16),
-            pltpu.VMEM((share, features), bf16),
+            pltpu.VMEM((replicas, capacity, upstream.shape[1]), bf16),
+            pltpu.VMEM((replicas, capacity, upstream.shape[1]), bf16),
             pltpu.VMEM((share, features), f32),
             pltpu.VMEM((2 * share, features), bf16),
             pltpu.VMEM((features, 2 * share), bf16),
@@ -554,7 +559,7 @@
         block_ids[None, :],
         member[:, None],
         member[None, :],
-        upstream.reshape(-1, features),
+        upstream.reshape(replicas, capacity, -1),
     )
     return (received.reshape(upstream.shape), grad_in, grad_out_t.T)
 

time: 129 us -> 126 us (0.977)
  local copies, waits for them, and re-layouts: 9.54 us -> 7.02 us
    reshape x2 -> x0, local copies, waits for them, and re-layouts: 4.49 us -> none  [the longest x1 2.25 us: in_one_kernel(): return (received.reshape(upstream.shape), grad_in, grad_out_t.T)]
    unnamed x2 -> x3, local copies, waits for them, and re-layouts: 3.56 us -> 5.52 us
where the time goes in v5:
time: 126 us
  Pallas kernels  117 us (93%)
  local copies, waits for them, and re-layouts  7.02 us (6%)
    pallas_call x1, Pallas kernels, in_one_kernel(): pl.pallas_call(functools.partial(window_kernel, sections, replicas, merge...  117 us
    unnamed x3, local copies, waits for them, and re-layouts  5.52 us

profile of v5, /device:TPU:0, one launch (start us, length us, event | category | flops | bytes accessed | tf_op | source)
XLA Modules:
  0.0 125.8 jit_solution(5561110128859733878)
XLA Ops:
  0.6 0.7 convert_bitcast_fusion
  1.3 0.1 broadcast_in_dim.2
  1.4 0.7 convert_element_type.32.trow
  2.0 0.7 convert_element_type.33.tcol
  2.8 117.4 %shard_map.139 = (bf16[8,8,5120]{2,1,0:T(8,128)(2,1)}, f32[160,640]{1,0:T(8,128)}, f32[160,640]{1,0:T(8,128)}) custom-call(bf16[1024,1280]{1,0:T(8,128)(2,1)} %patches.1, f32[1280]{0:T(1024)} %pre_gain.1, f32[1280]{0:T(1024)} %merge_gain.1, f32[1280]{0:T(1024)} %merge_bias.1, bf16[160,640]{1,0:T(8,128)(2,1)} %w_in.1, bf16[160,640]{1,0:T(8,128)(2,1)} %bitcast.9, ...), custom_call_target="tpu_custom_call" | custom-call | tf_op jit(solution)/shard_map/pallas_call | solution.py:493
  120.2 2.0 %copy.19 = bf16[64,5120]{1,0:T(8,128)(2,1)} copy(bf16[64,5120]{1,0:T(8,128)(2,1)} %bitcast.7) | data formatting | bytes 1310720
  122.2 1.8 %copy.20 = f32[160,640]{1,0:T(8,128)} copy(f32[160,640]{1,0:T(8,128)} %get-tuple-element.13) | data formatting | bytes 819200
  124.0 1.8 %copy.21 = f32[640,160]{0,1:T(8,128)} copy(f32[640,160]{0,1:T(8,128)} %bitcast.8) | data formatting | bytes 819200
